TPU v7x, 32 devices: a whole 2x2x4 slice. The times are simulated.
32 devices in a mesh: group: 8 (over z, y), section: 4 (over x, core).
Axes of the slice: x: 2, y: 2, z: 4, core: 2. Of those that a mesh axis runs over, the one named last changes fastest.
Arguments:
- embed_in: bfloat16 [32, 32, 1792], P(('group', 'section')), may hold values from -6 to 6
- clean_cache: bfloat16 [4, 32, 32, 1792], P('section', 'group'), may hold values from -6 to 6
- lengths: int32 [32, 5], P(('group', 'section')), may hold values from 1 to 24, 32 in all within a row
- patch_layer: int32 [32, 4], P(('group', 'section')), may hold values from 0 to 3
- patch_pos: int32 [32, 4], P(('group', 'section')), may hold values from 0 to 31
- answers: int32 [32, 4, 2], P(('group', 'section')), may hold values from 0 to 77823
- attn_gain: float32 [4, 1792], P('section'), may hold values from 0.5 to 1.5
- w_query: bfloat16 [4, 1792, 1792], P('section', 'group'), may hold values from -0.125 to 0.125
- b_query: float32 [4, 1792], P('section'), may hold values from -3 to 3
- w_keyval: bfloat16 [4, 1792, 512], P('section', 'group'), may hold values from -0.125 to 0.125
- b_key: float32 [4, 256], P('section'), may hold values from -3 to 3
- b_value: float32 [4, 256], P('section'), may hold values from -3 to 3
- w_out: bfloat16 [4, 1792, 1792], P('section', 'group'), may hold values from -0.125 to 0.125
- final_gain: float32 [1792], replicated, may hold values from 0.5 to 1.5
- unembed: bfloat16 [77824, 1792], P(('group', 'section')), may hold values from -0.125 to 0.125
Outputs:
- final_resid: bfloat16 [32, 32, 1792], P(('group', 'section'))
- logit_diff: float32 [32, 4], P(('group', 'section'))
- cell_sums: float32 [4, 24], replicated
Inputs may be any that keep to these rules, and one draw needn't show every extreme that they name: Each row holds 4 prompt lengths followed by the padding of its bucket and sums to 32.
All inputs are finite; a program needn't handle non-finite values.
Results may differ from a plain program's by a relative error of at most 0.02.
Values may be sent and summed in bfloat16 or wider, within the bound.
A program may use at most 128 MiB of HBM per device.

v0:
```python
import math

import jax
import jax.numpy as jnp
from jax import lax
from jax.sharding import PartitionSpec as P

HQ = 14
KV = 2
HD = 128
MAXLEN = 24


epsilon = 1e-06
rope_base = 1000000.0


def from_behind(block, axis, distance):
    devices = range(lax.axis_size(axis))
    route = [(i - distance, i) for i in devices if i - distance in devices]
    return lax.ppermute(block, axis, route)


def spread(block, axis, owner):
    block = jnp.where(lax.axis_index(axis) == owner, block, jnp.zeros_like(block))
    return lax.psum(block, axis)


def rmsnorm(hidden, norm_gain):
    residual = hidden.astype(jnp.float32)
    scaled = residual * lax.rsqrt(jnp.mean(residual * residual, axis=-1, keepdims=True) + epsilon)
    return (scaled * norm_gain).astype(jnp.bfloat16)


def rotary(heads, position):
    half_dim = heads.shape[-1] // 2
    frequency = jnp.exp(jnp.arange(half_dim, dtype=jnp.float32) * (-math.log(rope_base) / half_dim))
    angles = position.astype(jnp.float32)[:, None] * frequency[None, :]
    cosine = jnp.cos(angles)[:, None, :]
    sinus = jnp.sin(angles)[:, None, :]
    front_half = heads[..., :half_dim]
    back_half = heads[..., half_dim:]
    return jnp.concatenate(
        [front_half * cosine - back_half * sinus, back_half * cosine + front_half * sinus], axis=-1
    )


def bucket_layout(lengths_rows, seq_len):
    end_rows = jnp.cumsum(lengths_rows, axis=-1).astype(jnp.int32)
    starts = (end_rows - lengths_rows).astype(jnp.int32)
    row_ids = jnp.arange(seq_len, dtype=jnp.int32)
    segment = jnp.sum((row_ids[:, None] >= end_rows[..., None, :]).astype(jnp.int32), axis=-1)
    slots = jnp.arange(lengths_rows.shape[-1], dtype=jnp.int32)
    member = segment[..., :, None] == slots
    position = row_ids - jnp.sum(jnp.where(member, starts[..., None, :], 0), axis=-1)
    return (segment, position, starts)


def patch_hits(starts, lengths_rows, layers, offsets, layer_now, seq_len):
    prompts = layers.shape[-1]
    target = (starts[..., :prompts] + offsets % lengths_rows[..., :prompts]).astype(jnp.int32)
    row_ids = jnp.arange(seq_len, dtype=jnp.int32)
    return jnp.any(
        (row_ids[:, None] == target[..., None, :]) & (layers[..., None, :] == layer_now), axis=-1
    )


def attend_piece(
    hidden,
    norm_gain,
    query_weight,
    query_bias,
    keyval_weight,
    key_bias,
    value_bias,
    output_weight,
    seg_query,
    pos_query,
    seg_keys,
    row_start,
    key_cache,
    value_cache,
):
    count_rows = hidden.shape[0]
    normed = rmsnorm(hidden, norm_gain)
    queries = jnp.dot(normed, query_weight, preferred_element_type=jnp.float32) + query_bias
    keyval = jnp.dot(normed, keyval_weight, preferred_element_type=jnp.float32)
    width_kv = keyval.shape[1] // 2
    keys_rot = rotary(
        (keyval[:, :width_kv] + key_bias).reshape(count_rows, KV, HD), pos_query
    ).astype(jnp.bfloat16)
    values_new = (
        (keyval[:, width_kv:] + value_bias).reshape(count_rows, KV, HD).astype(jnp.bfloat16)
    )
    queries_rot = rotary(queries.reshape(count_rows, HQ, HD), pos_query).astype(jnp.bfloat16)
    queries_rot = queries_rot.reshape(count_rows, KV, HQ // KV, HD)
    key_cache = keys_rot
    value_cache = values_new
    scores = jnp.einsum(
        "qgrd,kgd->grqk", queries_rot, key_cache, preferred_element_type=jnp.float32
    ) * HD ** (-0.5)
    query_ids = row_start + jnp.arange(count_rows, dtype=jnp.int32)
    key_ids = jnp.arange(key_cache.shape[0], dtype=jnp.int32)
    allowed = (seg_query[:, None] == seg_keys[None, :]) & (key_ids[None, :] <= query_ids[:, None])
    scores = jnp.where(allowed, scores, -1e30)
    weights = jax.nn.softmax(scores, axis=-1).astype(jnp.bfloat16)
    attended = jnp.einsum(
        "grqk,kgd->qgrd", weights, value_cache, preferred_element_type=jnp.float32
    )
    attended = attended.astype(jnp.bfloat16).reshape(count_rows, HQ * HD)
    updated = hidden.astype(jnp.float32) + jnp.dot(
        attended, output_weight, preferred_element_type=jnp.float32
    )
    return (updated.astype(jnp.bfloat16), key_cache, value_cache)


def pass_on(hidden):
    return from_behind(hidden, "section", 1)


def answer_terms(readout_all, answer_ids, unembed, offset):
    logits = lax.dot_general(
        readout_all, unembed, (((1,), (1,)), ((), ())), preferred_element_type=jnp.float32
    )
    vocab_ids = offset + jnp.arange(unembed.shape[0], dtype=jnp.int32)
    choosing = (answer_ids[:, 0:1] == vocab_ids[None, :]).astype(jnp.float32) - (
        answer_ids[:, 1:2] == vocab_ids[None, :]
    ).astype(jnp.float32)
    return jnp.sum(logits * choosing, axis=1)


def cell_table(answer_diffs, cell_ids, cell_count):
    onehot = (cell_ids[:, None] == jnp.arange(cell_count, dtype=jnp.int32)[None, :]).astype(
        jnp.float32
    )
    return jnp.dot(answer_diffs, onehot, precision=lax.Precision.HIGHEST)


def per_device(
    embed_in,
    clean_cache,
    lengths,
    patch_layer,
    patch_pos,
    answers,
    attn_gain,
    w_query,
    b_query,
    w_keyval,
    b_key,
    b_value,
    w_out,
    final_gain,
    unembed,
):
    section_count = lax.axis_size("section")
    section_index = lax.axis_index("section")
    seq_len = embed_in.shape[1]
    feature_count = embed_in.shape[2]
    prompts = patch_layer.shape[1]
    inputs, lens_all, layer_all, offset_all = (
        lax.all_gather(embed_in, "section", axis=0, tiled=True),
        lax.all_gather(lengths, "section", axis=0, tiled=True),
        lax.all_gather(patch_layer, "section", axis=0, tiled=True),
        lax.all_gather(patch_pos, "section", axis=0, tiled=True),
    )
    query_weight, keyval_weight, output_weight = (
        lax.all_gather(w_query[0], "group", axis=0, tiled=True),
        lax.all_gather(w_keyval[0], "group", axis=0, tiled=True),
        lax.all_gather(w_out[0], "group", axis=0, tiled=True),
    )
    segment, position, starts = bucket_layout(lens_all, seq_len)
    hits = patch_hits(starts, lens_all, layer_all, offset_all, section_index, seq_len)
    pieces = 1
    piece_rows = seq_len // pieces
    piece_total = section_count * pieces
    tick_count = section_count + piece_total - 1
    key_cache = jnp.zeros((seq_len, KV, HD), jnp.bfloat16)
    value_cache = jnp.zeros((seq_len, KV, HD), jnp.bfloat16)
    finished = jnp.zeros((section_count, seq_len, feature_count), jnp.bfloat16)
    moving = jnp.zeros((piece_rows, feature_count), jnp.bfloat16)
    for moment in range(tick_count):
        piece_order = moment - section_index
        in_range = (piece_order >= 0) & (piece_order < piece_total)
        clamped = jnp.clip(piece_order, 0, piece_total - 1)
        bucket = clamped // pieces
        row_start = clamped % pieces * piece_rows
        fresh_rows = lax.dynamic_slice(
            inputs, (bucket, row_start, 0), (1, piece_rows, feature_count)
        )[0]
        current = jnp.where(section_index == 0, fresh_rows, moving)
        clean_rows = lax.dynamic_slice(
            clean_cache[0], (bucket, row_start, 0), (1, piece_rows, feature_count)
        )[0]
        patched = lax.dynamic_slice(hits, (bucket, row_start), (1, piece_rows))[0]
        current = jnp.where(patched[:, None], clean_rows, current)
        seg_keys = lax.dynamic_slice_in_dim(segment, bucket, 1, 0)[0]
        pos_bucket = lax.dynamic_slice_in_dim(position, bucket, 1, 0)[0]
        result, key_cache, value_cache = attend_piece(
            current,
            attn_gain[0],
            query_weight,
            b_query[0],
            keyval_weight,
            b_key[0],
            b_value[0],
            output_weight,
            seg_keys,
            pos_bucket,
            seg_keys,
            row_start,
            key_cache,
            value_cache,
        )
        stored = lax.dynamic_update_slice(finished, result[None], (bucket, row_start, 0))
        finished = jnp.where(in_range & (section_index == section_count - 1), stored, finished)
        if moment + 1 < tick_count:
            moving = pass_on(result)
    gathered = spread(finished, "section", section_count - 1)
    own_rows = lax.dynamic_slice_in_dim(gathered, section_index, 1, 0)
    own_lengths = lengths[0]
    own_starts = jnp.cumsum(own_lengths) - own_lengths
    last_rows = own_starts[:prompts] + own_lengths[:prompts] - 1
    readout = rmsnorm(own_rows[0][last_rows], final_gain)
    distance = own_lengths[:prompts] - 1 - patch_pos[0] % own_lengths[:prompts]
    cell_ids = patch_layer[0] * MAXLEN + distance
    cell_count = section_count * MAXLEN
    offset = lax.axis_index(("group", "section")) * unembed.shape[0]
    readout_all, answer_ids = (
        lax.all_gather(readout, ("group", "section"), axis=0, tiled=True),
        lax.all_gather(answers[0], ("group", "section"), axis=0, tiled=True),
    )
    partial_value = answer_terms(readout_all, answer_ids, unembed, offset)
    own_diff = lax.psum_scatter(
        partial_value, ("group", "section"), scatter_dimension=0, tiled=True
    )
    cell_totals = lax.psum(cell_table(own_diff, cell_ids, cell_count), ("group", "section"))
    return (own_rows, own_diff.reshape(1, prompts), cell_totals.reshape(section_count, MAXLEN))


def solution(mesh):
    placed = (
        P(("group", "section"), None, None),
        P("section", "group", None, None),
        P(("group", "section"), None),
        P(("group", "section"), None),
        P(("group", "section"), None),
        P(("group", "section"), None, None),
        P("section", None),
        P("section", "group", None),
        P("section", None),
        P("section", "group", None),
        P("section", None),
        P("section", None),
        P("section", "group", None),
        P(),
        P(("group", "section"), None),
    )
    return jax.shard_map(
        per_device,
        mesh=mesh,
        in_specs=placed,
        out_specs=(P(("group", "section"), None, None), P(("group", "section"), None), P()),
        check_vma=False,
    )
```

profile of v0, /device:TPU:0, one launch (start us, length us, event | category | flops | bytes accessed | tf_op | source)
XLA Modules:
  0.0 557.1 jit_solution(7848652835291296165)
XLA Ops:
  9.4 6.2 %all-gather.6 = s32[4,1,4]{2,1,0:T(1,128)S(1)} all-gather(s32[1,1,4]{2,1,0:T(1,128)} %bitcast.555), channel_id=1, replica_groups=mesh['group'=8,'section'=4] {'section'}, dimensions={0}, use_global_device_ids=true | all-gather | bytes 80 | tf_op jit(solution)/shard_map/all_gather | solution.py:164
  15.6 5.4 all-gather.5
  21.1 5.2 all-gather.4
  31.2 7.2 %all_gather.30 = bf16[4,32,1792]{2,1,0:T(8,128)(2,1)S(1)} all-gather(bf16[1,32,1792]{2,1,0:T(8,128)(2,1)} %param.15), channel_id=1, replica_groups=mesh['group'=8,'section'=4] {'section'}, dimensions={0}, use_global_device_ids=true | all-gather | bytes 573440 | tf_op jit(solution)/shard_map/all_gather | solution.py:162
  42.0 17.3 %all-gather.12.cloned.1.call-done = bf16[1,1792,512]{2,1,0:T(8,128)(2,1)} async-done(((bf16[1,224,512]{2,1,0:T(8,128)(2,1)}), bf16[1,1792,512]{2,1,0:T(8,128)(2,1)}) %all-gather.12.cloned.1.call-update) | async-done | bytes 1835024 | tf_op jit(solution)/shard_map/all_gather | solution.py:169
  59.3 2.0 fusion.119
  62.1 98.4 %all-gather.14.cloned.1.call-done = bf16[1,1792,1792]{2,1,0:T(8,128)(2,1)} async-done(((bf16[1,224,1792]{2,1,0:T(8,128)(2,1)}), bf16[1,1792,1792]{2,1,0:T(8,128)(2,1)}) %all-gather.14.cloned.1.call-update) | async-done | bytes 6422544 | tf_op jit(solution)/shard_map/all_gather | solution.py:168
  160.5 4.1 fusion.35
  166.1 95.1 %all-gather.16.cloned.1.call-done = bf16[1,1792,1792]{2,1,0:T(8,128)(2,1)} async-done(((bf16[1,224,1792]{2,1,0:T(8,128)(2,1)}), bf16[1,1792,1792]{2,1,0:T(8,128)(2,1)}) %all-gather.16.cloned.1.call-update) | async-done | bytes 6422544 | tf_op jit(solution)/shard_map/all_gather | solution.py:170
  261.3 4.0 bitcast_dynamic-update-slice_fusion
  270.5 4.1 fusion.38
  279.7 4.0 fusion.208
  283.8 4.9 collective-permute-start.1
  292.0 4.1 fusion.41
  299.8 4.0 fusion.206
  303.8 5.3 collective-permute-start.2
  312.3 4.1 fusion.44
  320.1 4.0 fusion.204
  324.2 5.2 collective-permute-start.3
  332.0 4.1 fusion.47
  339.1 4.0 fusion.202
  343.1 5.3 collective-permute-start.4
  351.1 4.1 fusion.50
  356.8 4.0 fusion.200
  360.9 5.5 collective-permute-start.5
  368.8 4.1 fusion.53
  374.5 4.0 fusion.104
  379.5 43.0 %all-gather.3 = s32[1,128,2]{2,0,1:T(1,128)S(1)} all-gather(s32[1,4,2]{2,0,1:T(1,128)S(1)} %copy.260), channel_id=5, replica_groups=mesh['group'=8,'section'=4] {'group','section'}, dimensions={1}, use_global_device_ids=true | all-gather | bytes 1056 | tf_op jit(solution)/shard_map/all_gather | solution.py:231
  424.4 37.9 %all-gather.7 = bf16[32,4,1792]{2,1,0:T(4,128)(2,1)S(1)} all-gather(bf16[1,4,1792]{2,1,0:T(4,128)(2,1)S(1)} %fusion.290), channel_id=1, replica_groups=mesh['group'=8,'section'=4] {'group','section'}, dimensions={0}, use_global_device_ids=true | all-gather | bytes 473088 | tf_op jit(solution)/shard_map/all_gather | solution.py:230
  462.4 6.4 %fusion.121 = f32[128]{0:T(128)S(1)} fusion(bf16[128,1792]{1,0:T(8,128)(2,1)S(1)} %reshape.735, bf16[2432,1792]{1,0:T(8,128)(2,1)} %param.29, s32[2432]{0:T(1024)S(1)} %iota_add_fusion, s32[128]{0:T(128)S(1)} %get-tuple-element.4, s32[128]{0:T(128)S(1)} %get-tuple-element.3), kind=kOutput, calls=%fused_computation.75 | convolution fusion | flops 1117863808 | bytes 9186304 | tf_op jit(solution)/shard_map/dot_general | solution.py:122
  468.9 36.9 %all-reduce = f32[128]{0:T(128)S(1)} all-reduce(f32[128]{0:T(128)S(1)} %fusion.121), channel_id=6, replica_groups=mesh['group'=8,'section'=4] {'group','section'}, use_global_device_ids=true, to_apply=%region_29.30.clone | all-reduce | flops 128 | bytes 1024
  506.7 42.3 %psum.15 = f32[4,24]{1,0:T(4,128)} all-reduce(f32[4,24]{1,0:T(4,128)S(1)} %reshape.714), channel_id=1, replica_groups=mesh['group'=8,'section'=4] {'group','section'}, use_global_device_ids=true, to_apply=%region_30.31 | all-reduce | flops 96 | bytes 768 | tf_op jit(solution)/shard_map/psum | solution.py:237
  (230 shorter events, 55.6 us)
Async XLA Ops:
  7.2 52.1 %all-gather.12.cloned.1.call-start = ((), (), s32[]{:S(2)}) async-start(), calls=%async_computation.1 | async-start | bytes 2064384 | tf_op jit(solution)/shard_map/all_gather | solution.py:169
  7.9 152.6 %all-gather.14.cloned.1.call-start = ((), (), s32[]{:S(2)}) async-start(), calls=%async_computation.2 | async-start | bytes 7225344 | tf_op jit(solution)/shard_map/all_gather | solution.py:168
  8.6 252.6 %all-gather.16.cloned.1.call-start = ((), (), s32[]{:S(2)}) async-start(), calls=%async_computation.3 | async-start | bytes 7225344 | tf_op jit(solution)/shard_map/all_gather | solution.py:170
  9.4 413.3 %all-reduce.3.cloned.1.call-start = ((), (), s32[]{:S(2)}) async-start(), calls=%async_computation | async-start | bytes 917504 | tf_op jit(solution)/shard_map/psum | solution.py:26
  164.6 104.1 %copy-start = (bf16[1,1792,512]{2,1,0:T(8,128)(2,1)S(1)}, bf16[1,1792,512]{2,1,0:T(8,128)(2,1)}, u32[]{:S(2)}) copy-start(bf16[1,1792,512]{2,1,0:T(8,128)(2,1)} %all-gather.12.cloned.1.call-done) | copy-start | bytes 5505028
  164.9 104.3 %copy-start.1 = (f32[1,256]{1,0:T(1,128)S(1)}, f32[1,256]{1,0:T(1,128)}, u32[]{:S(2)}) copy-start(f32[1,256]{1,0:T(1,128)} %param.26) | copy-start | bytes 3076
  164.9 104.3 %copy-start.7 = (f32[1,256]{1,0:T(1,128)S(1)}, f32[1,256]{1,0:T(1,128)}, u32[]{:S(2)}) copy-start(f32[1,256]{1,0:T(1,128)} %param.25) | copy-start | bytes 3076
  265.3 2.2 collective-permute-start
  274.7 14.0 %copy-start.16 = (s32[32]{0:T(128)S(1)}, s32[32]{0:T(128)}, u32[]{:S(2)}) copy-start(s32[32]{0:T(128)} %get-tuple-element.77) | copy-start | bytes 388
  274.7 15.0 %copy-start.23 = (pred[32]{0:T(512)(128)(4,1)S(1)}, pred[32]{0:T(512)(128)(4,1)}, u32[]{:S(2)}) copy-start(pred[32]{0:T(512)(128)(4,1)} %get-tuple-element.121) | copy-start | bytes 100
  275.6 15.7 %copy-start.2 = (f32[1,256]{1,0:T(1,128)S(1)}, f32[1,256]{1,0:T(1,128)}, u32[]{:S(2)}) copy-start(f32[1,256]{1,0:T(1,128)} %param.26) | copy-start | bytes 3076
  275.6 15.7 %copy-start.8 = (f32[1,256]{1,0:T(1,128)S(1)}, f32[1,256]{1,0:T(1,128)}, u32[]{:S(2)}) copy-start(f32[1,256]{1,0:T(1,128)} %param.25) | copy-start | bytes 3076
  283.8 5.9 %collective-permute-start.1 = (bf16[32,1792]{1,0:T(8,128)(2,1)S(1)}, bf16[32,1792]{1,0:T(8,128)(2,1)S(1)}, u32[]{:S(2)}, u32[]{:S(2)}) collective-permute-start(bf16[32,1792]{1,0:T(8,128)(2,1)S(1)} %get-tuple-element.127), channel_id=1, source_target_pairs={{0,1},{1,2},{2,3},{4,5},{5,6},{6,7},{8,9},{9,10},{10,11},{12,13},{... | collective-permute-start | bytes 344072 | tf_op jit(solution)/shard_map/ppermute | solution.py:21
  296.2 13.0 %copy-start.15 = (s32[32]{0:T(128)S(1)}, s32[32]{0:T(128)}, u32[]{:S(2)}) copy-start(s32[32]{0:T(128)} %get-tuple-element.76) | copy-start | bytes 388
  296.2 13.8 %copy-start.22 = (pred[32]{0:T(512)(128)(4,1)S(1)}, pred[32]{0:T(512)(128)(4,1)}, u32[]{:S(2)}) copy-start(pred[32]{0:T(512)(128)(4,1)} %get-tuple-element.120) | copy-start | bytes 100
  296.4 15.2 %copy-start.3 = (f32[1,256]{1,0:T(1,128)S(1)}, f32[1,256]{1,0:T(1,128)}, u32[]{:S(2)}) copy-start(f32[1,256]{1,0:T(1,128)} %param.26) | copy-start | bytes 3076
  296.4 15.2 %copy-start.9 = (f32[1,256]{1,0:T(1,128)S(1)}, f32[1,256]{1,0:T(1,128)}, u32[]{:S(2)}) copy-start(f32[1,256]{1,0:T(1,128)} %param.25) | copy-start | bytes 3076
  303.8 6.1 %collective-permute-start.2 = (bf16[32,1792]{1,0:T(8,128)(2,1)S(1)}, bf16[32,1792]{1,0:T(8,128)(2,1)S(1)}, u32[]{:S(2)}, u32[]{:S(2)}) collective-permute-start(bf16[32,1792]{1,0:T(8,128)(2,1)S(1)} %get-tuple-element.129), channel_id=1, source_target_pairs={{0,1},{1,2},{2,3},{4,5},{5,6},{6,7},{8,9},{9,10},{10,11},{12,13},{... | collective-permute-start | bytes 344072 | tf_op jit(solution)/shard_map/ppermute | solution.py:21
  316.5 12.9 %copy-start.14 = (s32[32]{0:T(128)S(1)}, s32[32]{0:T(128)}, u32[]{:S(2)}) copy-start(s32[32]{0:T(128)} %get-tuple-element.75) | copy-start | bytes 388
  316.5 13.8 %copy-start.21 = (pred[32]{0:T(512)(128)(4,1)S(1)}, pred[32]{0:T(512)(128)(4,1)}, u32[]{:S(2)}) copy-start(pred[32]{0:T(512)(128)(4,1)} %get-tuple-element.119) | copy-start | bytes 100
  316.7 15.2 %copy-start.4 = (f32[1,256]{1,0:T(1,128)S(1)}, f32[1,256]{1,0:T(1,128)}, u32[]{:S(2)}) copy-start(f32[1,256]{1,0:T(1,128)} %param.26) | copy-start | bytes 3076
  316.7 15.2 %copy-start.10 = (f32[1,256]{1,0:T(1,128)S(1)}, f32[1,256]{1,0:T(1,128)}, u32[]{:S(2)}) copy-start(f32[1,256]{1,0:T(1,128)} %param.25) | copy-start | bytes 3076
  324.2 6.1 %collective-permute-start.3 = (bf16[32,1792]{1,0:T(8,128)(2,1)S(1)}, bf16[32,1792]{1,0:T(8,128)(2,1)S(1)}, u32[]{:S(2)}, u32[]{:S(2)}) collective-permute-start(bf16[32,1792]{1,0:T(8,128)(2,1)S(1)} %get-tuple-element.131), channel_id=1, source_target_pairs={{0,1},{1,2},{2,3},{4,5},{5,6},{6,7},{8,9},{9,10},{10,11},{12,13},{... | collective-permute-start | bytes 344072 | tf_op jit(solution)/shard_map/ppermute | solution.py:21
  336.2 13.2 %copy-start.20 = (pred[32]{0:T(512)(128)(4,1)S(1)}, pred[32]{0:T(512)(128)(4,1)}, u32[]{:S(2)}) copy-start(pred[32]{0:T(512)(128)(4,1)} %get-tuple-element.118) | copy-start | bytes 100
  336.4 14.6 %copy-start.5 = (f32[1,256]{1,0:T(1,128)S(1)}, f32[1,256]{1,0:T(1,128)}, u32[]{:S(2)}) copy-start(f32[1,256]{1,0:T(1,128)} %param.26) | copy-start | bytes 3076
  336.4 14.6 %copy-start.11 = (f32[1,256]{1,0:T(1,128)S(1)}, f32[1,256]{1,0:T(1,128)}, u32[]{:S(2)}) copy-start(f32[1,256]{1,0:T(1,128)} %param.25) | copy-start | bytes 3076
  343.1 12.5 %copy-start.18 = (pred[32,32]{0,1:T(8,128)(4,1)S(1)}, pred[32,32]{0,1:T(8,128)(4,1)}, u32[]{:S(2)}) copy-start(pred[32,32]{0,1:T(8,128)(4,1)} %fusion.284) | copy-start | bytes 3076
  343.1 6.2 %collective-permute-start.4 = (bf16[32,1792]{1,0:T(8,128)(2,1)S(1)}, bf16[32,1792]{1,0:T(8,128)(2,1)S(1)}, u32[]{:S(2)}, u32[]{:S(2)}) collective-permute-start(bf16[32,1792]{1,0:T(8,128)(2,1)S(1)} %get-tuple-element.133), channel_id=1, source_target_pairs={{0,1},{1,2},{2,3},{4,5},{5,6},{6,7},{8,9},{9,10},{10,11},{12,13},{... | collective-permute-start | bytes 344072 | tf_op jit(solution)/shard_map/ppermute | solution.py:21
  355.5 13.2 %copy-start.6 = (f32[1,256]{1,0:T(1,128)S(1)}, f32[1,256]{1,0:T(1,128)}, u32[]{:S(2)}) copy-start(f32[1,256]{1,0:T(1,128)} %param.26) | copy-start | bytes 3076
  355.5 13.2 %copy-start.12 = (f32[1,256]{1,0:T(1,128)S(1)}, f32[1,256]{1,0:T(1,128)}, u32[]{:S(2)}) copy-start(f32[1,256]{1,0:T(1,128)} %param.25) | copy-start | bytes 3076
  360.9 6.2 %collective-permute-start.5 = (bf16[32,1792]{1,0:T(8,128)(2,1)S(1)}, bf16[32,1792]{1,0:T(8,128)(2,1)S(1)}, u32[]{:S(2)}, u32[]{:S(2)}) collective-permute-start(bf16[32,1792]{1,0:T(8,128)(2,1)S(1)} %get-tuple-element.135), channel_id=1, source_target_pairs={{0,1},{1,2},{2,3},{4,5},{5,6},{6,7},{8,9},{9,10},{10,11},{12,13},{... | collective-permute-start | bytes 344072 | tf_op jit(solution)/shard_map/ppermute | solution.py:21
  373.0 51.3 %copy-start.13 = (f32[1792]{0:T(1024)S(1)}, f32[1792]{0:T(1024)}, u32[]{:S(2)}) copy-start(f32[1792]{0:T(1024)} %param.28) | copy-start | bytes 21508
  (8 other events, 88.8 us)
Sparse Core Ops, SparseCore 0:
  10.2 49.0 all-gather.11
  61.5 98.9 all-gather.13
  162.7 98.4 all-gather.15
  379.5 35.3 all-reduce.2
where the time goes:
time: 559 us; the launch traced here: 557 us
  waiting for transfers between devices  215 us (38%)
  blocking collectives  184 us (33%)
  matrix products  80.4 us (14%)
  starting transfers between devices  27.7 us (5%)
  other arithmetic  23.9 us (4%)
  between operations  14.8 us (3%)
  local copies, waits for them, and re-layouts  10.8 us (2%)
    all_gather x1, waiting for transfers between devices, per_device(): lax.all_gather(w_query[0], 'group', axis=0, tiled=True)  98.4 us
    all_gather x1, waiting for transfers between devices, per_device(): lax.all_gather(w_out[0], 'group', axis=0, tiled=True)  95.1 us
    all_gather x1, blocking collectives, per_device(): lax.all_gather(answers[0], ('group', 'section'), axis=0, tiled=True)  43 us
    psum x1, blocking collectives, per_device(): lax.psum(cell_table(own_diff, cell_ids, cell_count), ('group', 'section'))  42.3 us
    all_gather x1, blocking collectives, per_device(): lax.all_gather(readout, ('group', 'section'), axis=0, tiled=True)  37.9 us
    unnamed x1, blocking collectives  36.9 us
    dot_general x7, matrix products, attend_piece(): jnp.dot(normed, query_weight, preferred_element_type=jnp.float32)  28.7 us
    dot_general x7, matrix products, attend_piece(): jnp.dot(attended, output_weight, preferred_element_type=jnp.float32)  28.3 us
  transfers between devices with their start and end apart: 10, of which 9 were waited for; matrix products, arithmetic and copies ran while one was open for 4% of the time, Pallas kernels for 0%

commit v1 on v0

v1 whole, which is shorter than its diff:
```python
import functools
import math

import jax
import jax.numpy as jnp
from jax import lax
from jax.experimental import pallas as pl
from jax.experimental.pallas import tpu as pltpu
from jax.sharding import PartitionSpec as P

HD = 128
MAXLEN = 24
EPS = 1e-06
ROPE_BASE = 1000000.0
MESH = pl.DeviceIdType.MESH
TILE = 256
STAT = 8


def rms(rows, gain):
    x = rows.astype(jnp.float32)
    scaled = x * lax.rsqrt(jnp.mean(x * x, axis=-1, keepdims=True) + EPS)
    return (scaled * gain).astype(jnp.bfloat16)


def ring_group(place, n):
    late = place // (n // 2)
    return (1 - late) * 2 * place + late * (2 * (n - 1 - place) + 1)


def window_kernel(
    n,
    ns,
    ring,
    embed,
    wq,
    wkv,
    wo,
    terms,
    clean,
    hit,
    mask,
    cosine,
    sinus,
    gain,
    bq,
    bk,
    bv,
    final_gain,
    pick,
    cells,
    rows_out,
    stats_out,
    wq_all,
    wkv_all,
    wo_all,
    h_in,
    h_out,
    normed,
    q_rot,
    k_rot,
    v_all,
    att,
    term_buf,
    stat,
    w_send,
    w_recv,
    w_local,
    e_send,
    e_recv,
    t_send,
    t_recv,
    t_local,
    h_send,
    h_recv,
    r_send,
    r_recv,
    s_send,
    s_recv,
):
    g = lax.axis_index("group")
    s = lax.axis_index("section")
    total = n * ns
    me = g * ns + s
    last = ns - 1
    bucket = embed.shape[0]
    d = embed.shape[1]
    width = wq_all.shape[1]
    kvw = wkv_all.shape[1] // 2
    kv_heads = kvw // HD
    heads = width // HD
    per = heads // kv_heads

    barrier = pltpu.get_barrier_semaphore()

    def greet(i, c):
        t = lax.rem(me + i, total)
        pl.semaphore_signal(barrier, inc=1, device_id=(t // ns, lax.rem(t, ns)), device_id_type=MESH)
        return c

    lax.fori_loop(1, total, greet, 0)
    pl.semaphore_wait(barrier, total - 1)

    ins = (wq, wkv, wo)
    alls = (wq_all, wkv_all, wo_all)
    shard = wq.shape[0]
    if ring:
        odd = lax.rem(g, 2)
        place = (1 - odd) * (g // 2) + odd * (n - 1 - g // 2)
        right = ring_group(lax.rem(place + 1, n), n)
        left = ring_group(lax.rem(place + n - 1, n), n)
        half = n // 2

        def rows_of(step, way):
            at = lax.rem(place + n - step, n) if way == 0 else lax.rem(place + step, n)
            return pl.ds(pl.multiple_of(ring_group(at, n) * shard, shard), shard)

        def hop(step, way, a):
            rows = rows_of(step, way)
            src = ins[a] if step == 0 else alls[a].at[rows]
            return pltpu.make_async_remote_copy(
                src_ref=src,
                dst_ref=alls[a].at[rows],
                send_sem=w_send.at[way, step, a],
                recv_sem=w_recv.at[way, step, a],
                device_id=((right, left)[way], s),
                device_id_type=MESH,
            )

        def used(step, way, a):
            if step < half - 1:
                return True
            return (a == 0) if way == 0 else (a != 0)

        for a in range(3):
            for way in range(2):
                if used(0, way, a):
                    hop(0, way, a).start()
        own = pl.ds(pl.multiple_of(g * shard, shard), shard)
    else:
        own = pl.ds(0, shard)
    local = [
        pltpu.make_async_copy(ins[a], alls[a].at[own], w_local.at[a]) for a in range(3)
    ]
    for copy in local:
        copy.start()

    own_rows = pl.ds(pl.multiple_of(s * bucket, bucket), bucket)
    e_out = pltpu.make_async_remote_copy(
        src_ref=embed,
        dst_ref=h_in.at[own_rows],
        send_sem=e_send,
        recv_sem=e_recv.at[s],
        device_id=(g, 0),
        device_id_type=MESH,
    )
    e_own = pltpu.make_async_copy(embed, h_in.at[own_rows], e_send)

    @pl.when(s != 0)
    def _():
        e_out.start()

    @pl.when(s == 0)
    def _():
        e_own.start()

    def term_copy(i, slot):
        t = lax.rem(g + i, n)
        return pltpu.make_async_remote_copy(
            src_ref=terms.at[t],
            dst_ref=term_buf.at[slot],
            send_sem=t_send.at[i],
            recv_sem=t_recv.at[slot],
            device_id=(t, last),
            device_id_type=MESH,
        )

    def send_term(i, c):
        term_copy(i, me).start()
        return c

    t_own = pltpu.make_async_copy(terms.at[g], term_buf.at[me], t_local)

    @pl.when(s == last)
    def _():
        t_own.start()

    @pl.when(s != last)
    def _():
        term_copy(0, me).start()

    lax.fori_loop(1, n, send_term, 0)

    if ring:
        for step in range(1, half):
            for a in range(3):
                for way in range(2):
                    hop(step - 1, way, a).wait_recv()
                    if used(step, way, a):
                        hop(step, way, a).start()
        for a in range(3):
            for way in range(2):
                if used(half - 1, way, a):
                    hop(half - 1, way, a).wait_recv()
        for step in range(half):
            for a in range(3):
                for way in range(2):
                    if used(step, way, a):
                        hop(step, way, a).wait_send()
    for copy in local:
        copy.wait()

    h_copy = pltpu.make_async_remote_copy(
        src_ref=h_out,
        dst_ref=h_in,
        send_sem=h_send,
        recv_sem=h_recv,
        device_id=(g, lax.rem(s + 1, ns)),
        device_id_type=MESH,
    )

    @pl.when(s == 0)
    def _():
        e_own.wait()
        for i in range(1, ns):
            rows = pl.ds(i * bucket, bucket)
            pltpu.make_async_remote_copy(
                src_ref=embed,
                dst_ref=h_in.at[rows],
                send_sem=e_send,
                recv_sem=e_recv.at[i],
                device_id=(g, 0),
                device_id_type=MESH,
            ).wait_recv()

    @pl.when(s != 0)
    def _():
        e_out.wait_send()
        h_copy.wait_recv()

    h_in[...] = jnp.where(hit[...] > 0, clean[...], h_in[...])
    normed[...] = rms(h_in[...], gain[...])
    cos_t = cosine[...]
    sin_t = sinus[...]

    def rotate(x):
        return (x * cos_t + pltpu.roll(x, HD // 2, 1) * sin_t).astype(jnp.bfloat16)

    keys = jnp.dot(normed[...], wkv_all[:, :kvw], preferred_element_type=jnp.float32) + bk[...]
    for k in range(kv_heads):
        k_rot[k] = rotate(keys[:, k * HD : (k + 1) * HD])
    values = jnp.dot(normed[...], wkv_all[:, kvw:], preferred_element_type=jnp.float32) + bv[...]
    v_all[...] = values.astype(jnp.bfloat16)

    def query_tile(t, c):
        cols = pl.ds(pl.multiple_of(t * TILE, TILE), TILE)
        q = jnp.dot(normed[...], wq_all[:, cols], preferred_element_type=jnp.float32) + bq[:, cols]
        for k in range(TILE // HD):
            q_rot[t * (TILE // HD) + k] = rotate(q[:, k * HD : (k + 1) * HD])
        return c

    lax.fori_loop(0, width // TILE, query_tile, 0)
    rows_all = h_in.shape[0]
    open_ = mask[...] > 0
    for h in range(heads):
        k = h // per
        sc = lax.dot_general(
            q_rot[h], k_rot[k], (((1,), (1,)), ((), ())), preferred_element_type=jnp.float32
        ) * HD ** (-0.5)
        sc = jnp.where(open_, sc, -1e30)
        ex = jnp.exp(sc - jnp.max(sc, axis=-1, keepdims=True))
        w = (ex / jnp.sum(ex, axis=-1, keepdims=True)).astype(jnp.bfloat16)
        att[:, h * HD : (h + 1) * HD] = jnp.dot(
            w, v_all[:, k * HD : (k + 1) * HD], preferred_element_type=jnp.float32
        ).astype(jnp.bfloat16)

    def out_tile(t, c):
        cols = pl.ds(pl.multiple_of(t * TILE, TILE), TILE)
        up = jnp.dot(att[...], wo_all[:, cols], preferred_element_type=jnp.float32)
        h_out[:, cols] = (h_in[:, cols].astype(jnp.float32) + up).astype(jnp.bfloat16)
        return c

    lax.fori_loop(0, d // TILE, out_tile, 0)

    @pl.when(s != last)
    def _():
        h_copy.start()

    def row_copy(i):
        return pltpu.make_async_remote_copy(
            src_ref=h_out.at[pl.ds(i * bucket, bucket)],
            dst_ref=rows_out,
            send_sem=r_send.at[i],
            recv_sem=r_recv,
            device_id=(g, i),
            device_id_type=MESH,
        )

    def stat_copy(i, slot):
        t = lax.rem(me + i, total)
        return pltpu.make_async_remote_copy(
            src_ref=stat,
            dst_ref=stats_out.at[slot],
            send_sem=s_send.at[i],
            recv_sem=s_recv.at[slot],
            device_id=(t // ns, lax.rem(t, ns)),
            device_id_type=MESH,
        )

    def wait_stat(slot):
        stat_copy(1, slot).wait_recv()

    @pl.when(s == last)
    def _():
        for i in range(last):
            row_copy(i).start()
        row_own = pltpu.make_async_copy(
            h_out.at[pl.ds(last * bucket, bucket)], rows_out, r_send.at[last]
        )
        row_own.start()

        t_own.wait()

        def take_term(i, c):
            term_copy(1, lax.rem(me + i, total)).wait_recv()
            return c

        lax.fori_loop(1, total, take_term, 0)

        def add_term(i, acc):
            return acc + term_buf[i].astype(jnp.float32)

        diff_rows = lax.fori_loop(1, total, add_term, term_buf[0].astype(jnp.float32))
        picked = jnp.dot(pick[...], h_out[...], preferred_element_type=jnp.float32)
        readout = rms(picked, final_gain[...]).astype(jnp.float32)
        diffs = jnp.sum(readout * diff_rows, axis=-1, keepdims=True)
        stat[STAT:, :] = jnp.broadcast_to(diffs, (stat.shape[0] - STAT, HD))
        stat[:STAT, :] = jnp.broadcast_to(
            jnp.sum(diffs * cells[...], axis=0, keepdims=True), (STAT, HD)
        )
        s_own = pltpu.make_async_copy(stat, stats_out.at[g], s_send.at[0])
        s_own.start()

        def send_stat(i, c):
            stat_copy(i, g).start()
            return c

        lax.fori_loop(1, total, send_stat, 0)

        def others(i, c):
            wait_stat(lax.rem(g + i, n))
            return c

        lax.fori_loop(1, n, others, 0)

        def sent(i, c):
            stat_copy(i, g).wait_send()
            return c

        lax.fori_loop(1, total, sent, 0)
        s_own.wait()
        row_own.wait()
        for i in range(last):
            row_copy(i).wait_send()

    @pl.when(s != last)
    def _():
        h_copy.wait_send()
        term_copy(0, me).wait_send()
        row_copy(0).wait_recv()

        def every(i, c):
            wait_stat(i)
            return c

        lax.fori_loop(0, n, every, 0)

    def term_sent(i, c):
        term_copy(i, me).wait_send()
        return c

    lax.fori_loop(1, n, term_sent, 0)


def bucket_layout(lengths_rows, seq_len):
    end_rows = jnp.cumsum(lengths_rows, axis=-1).astype(jnp.int32)
    starts = (end_rows - lengths_rows).astype(jnp.int32)
    row_ids = jnp.arange(seq_len, dtype=jnp.int32)
    segment = jnp.sum((row_ids[:, None] >= end_rows[..., None, :]).astype(jnp.int32), axis=-1)
    slots = jnp.arange(lengths_rows.shape[-1], dtype=jnp.int32)
    member = segment[..., :, None] == slots
    position = row_ids - jnp.sum(jnp.where(member, starts[..., None, :], 0), axis=-1)
    return (segment, position, starts)


def per_device(
    n,
    ns,
    embed_in,
    clean_cache,
    lengths,
    patch_layer,
    patch_pos,
    answers,
    attn_gain,
    w_query,
    b_query,
    w_keyval,
    b_key,
    b_value,
    w_out,
    final_gain,
    unembed,
):
    g = lax.axis_index("group")
    s = lax.axis_index("section")
    seq_len, d = embed_in.shape[1:]
    prompts = patch_layer.shape[1]
    entries = lengths.shape[1]
    width = w_query.shape[2]
    kvw = b_key.shape[1]
    rows_all = ns * seq_len
    total = n * ns

    packed = jnp.concatenate(
        [lengths, patch_layer, patch_pos, answers.reshape(1, 2 * prompts)], axis=1
    )
    table = lax.all_gather(packed, ("group", "section"), axis=0, tiled=True)
    at = entries + 2 * prompts
    answer_ids = table[:, at:].reshape(total * prompts, 2)
    mine = lax.dynamic_slice_in_dim(table, g * ns, ns, 0)
    lens = mine[:, :entries]
    layers = mine[:, entries : entries + prompts]
    offsets = mine[:, entries + prompts : at]

    vocab_ids = (g * ns + s) * unembed.shape[0] + jnp.arange(unembed.shape[0], dtype=jnp.int32)
    choosing = (answer_ids[:, 0:1] == vocab_ids[None, :]).astype(jnp.bfloat16) - (
        answer_ids[:, 1:2] == vocab_ids[None, :]
    ).astype(jnp.bfloat16)
    terms = jnp.dot(choosing, unembed, preferred_element_type=jnp.float32).astype(jnp.bfloat16)
    terms = terms.reshape(n, ns * prompts, d)

    segment, position, starts = bucket_layout(lens, seq_len)
    row_ids = jnp.arange(seq_len, dtype=jnp.int32)
    folded = offsets % lens[:, :prompts]
    target = starts[:, :prompts] + folded
    hit = jnp.any(
        (row_ids[:, None] == target[:, None, :]) & (layers[:, None, :] == s), axis=-1
    )
    hit = hit.reshape(rows_all, 1).astype(jnp.float32)
    ident = (segment + jnp.arange(ns, dtype=jnp.int32)[:, None] * entries).reshape(rows_all)
    all_rows = jnp.arange(rows_all, dtype=jnp.int32)
    mask = (
        (ident[:, None] == ident[None, :]) & (all_rows[None, :] <= all_rows[:, None])
    ).astype(jnp.float32)
    half = HD // 2
    frequency = jnp.exp(jnp.arange(half, dtype=jnp.float32) * (-math.log(ROPE_BASE) / half))
    angles = position.reshape(rows_all, 1).astype(jnp.float32) * frequency[None, :]
    cos_h = jnp.cos(angles)
    sin_h = jnp.sin(angles)
    cosine = jnp.concatenate([cos_h, cos_h], axis=1)
    sinus = jnp.concatenate([-sin_h, sin_h], axis=1)

    ends = starts[:, :prompts] + lens[:, :prompts] - 1
    last_rows = (ends + jnp.arange(ns, dtype=jnp.int32)[:, None] * seq_len).reshape(-1)
    pick = (last_rows[:, None] == all_rows[None, :]).astype(jnp.bfloat16)
    distance = lens[:, :prompts] - 1 - folded
    cell_ids = (layers * MAXLEN + distance).reshape(-1)
    cells = (cell_ids[:, None] == jnp.arange(HD, dtype=jnp.int32)[None, :]).astype(jnp.float32)

    wq, wkv, wo = w_query[0], w_keyval[0], w_out[0]
    ring = n % 2 == 0 and n > 2 and wq.shape[0] % 16 == 0
    if not ring:
        wq, wkv, wo = (lax.all_gather(w, "group", axis=0, tiled=True) for w in (wq, wkv, wo))
    hops = max(n // 2, 1) if ring else 1
    any_ = pl.BlockSpec(memory_space=pl.ANY)
    vmem = pl.BlockSpec(memory_space=pltpu.VMEM)
    dma = pltpu.SemaphoreType.DMA
    stat_rows = STAT + ns * prompts
    rows, stats = pl.pallas_call(
        functools.partial(window_kernel, n, ns, ring),
        out_shape=(
            jax.ShapeDtypeStruct((seq_len, d), jnp.bfloat16),
            jax.ShapeDtypeStruct((n, stat_rows, HD), jnp.float32),
        ),
        in_specs=[any_] * 5 + [vmem] * 12,
        out_specs=(vmem, vmem),
        scratch_shapes=[
            pltpu.VMEM((d, width), jnp.bfloat16),
            pltpu.VMEM((d, 2 * kvw), jnp.bfloat16),
            pltpu.VMEM((width, d), jnp.bfloat16),
            pltpu.VMEM((rows_all, d), jnp.bfloat16),
            pltpu.VMEM((rows_all, d), jnp.bfloat16),
            pltpu.VMEM((rows_all, d), jnp.bfloat16),
            pltpu.VMEM((width // HD, rows_all, HD), jnp.bfloat16),
            pltpu.VMEM((kvw // HD, rows_all, HD), jnp.bfloat16),
            pltpu.VMEM((rows_all, kvw), jnp.bfloat16),
            pltpu.VMEM((rows_all, width), jnp.bfloat16),
            pltpu.VMEM((total, ns * prompts, d), jnp.bfloat16),
            pltpu.VMEM((stat_rows, HD), jnp.float32),
            dma((2, hops, 3)),
            dma((2, hops, 3)),
            dma((3,)),
            dma,
            dma((ns,)),
            dma((n,)),
            dma((total,)),
            dma,
            dma,
            dma,
            dma((ns,)),
            dma,
            dma((total,)),
            dma((n,)),
        ],
        compiler_params=pltpu.CompilerParams(
            collective_id=0, has_side_effects=True, vmem_limit_bytes=60 * 1024 * 1024
        ),
    )(
        embed_in[0],
        wq,
        wkv,
        wo,
        terms,
        clean_cache[0].reshape(rows_all, d),
        hit,
        mask,
        cosine,
        sinus,
        attn_gain,
        b_query,
        b_key,
        b_value,
        final_gain[None, :],
        pick,
        cells,
    )
    totals = jnp.sum(stats[:, 0, :], axis=0)[: ns * MAXLEN].reshape(ns, MAXLEN)
    group_diffs = lax.dynamic_slice_in_dim(stats, g, 1, 0)[0, STAT:, 0]
    diffs = lax.dynamic_slice_in_dim(group_diffs, s * prompts, prompts, 0)
    return (rows[None], diffs[None, :], totals)


def solution(mesh):
    placed = (
        P(("group", "section"), None, None),
        P("section", "group", None, None),
        P(("group", "section"), None),
        P(("group", "section"), None),
        P(("group", "section"), None),
        P(("group", "section"), None, None),
        P("section", None),
        P("section", "group", None),
        P("section", None),
        P("section", "group", None),
        P("section", None),
        P("section", None),
        P("section", "group", None),
        P(),
        P(("group", "section"), None),
    )
    return jax.shard_map(
        functools.partial(per_device, mesh.shape["group"], mesh.shape["section"]),
        mesh=mesh,
        in_specs=placed,
        out_specs=(P(("group", "section"), None, None), P(("group", "section"), None), P()),
        check_vma=False,
    )
```

time: 559 us -> 275 us (0.49)
  waiting for transfers between devices: 215 us -> 0 us
  Pallas kernels: 0 us -> 213 us
  blocking collectives: 184 us -> 43.3 us
  matrix products: 80.4 us -> 5.68 us
  starting transfers between devices: 27.7 us -> 0 us
  other arithmetic: 23.9 us -> 4.81 us
  between operations: 14.8 us -> 0.7 us
    pallas_call x0 -> x1, Pallas kernels: none -> 213 us  [per_device(): pl.pallas_call(functools.partial(window_kernel, n, ns, ring), out_shape=(...]
    all_gather x3 -> x0, waiting for transfers between devices: 211 us -> none  [the longest x1 98.4 us: per_device(): lax.all_gather(w_query[0], 'group', axis=0, tiled=True)]
    dot_general x30 -> x1, matrix products: 75.1 us -> 5.68 us  [per_device(): jnp.dot(choosing, unembed, preferred_element_type=jnp.float32)]
    all_gather x6 -> x1, blocking collectives: 105 us -> 43.3 us  [per_device(): table = lax.all_gather(packed, ('group', 'section'), axis=0, tiled=True)]
    psum x1 -> x0, blocking collectives: 42.3 us -> none  [per_device(): lax.psum(cell_table(own_diff, cell_ids, cell_count), ('group', 'section'))]
    unnamed x1 -> x0, blocking collectives: 36.9 us -> none
    ppermute x6 -> x0, starting transfers between devices: 27.5 us -> none  [from_behind(): return lax.ppermute(block, axis, route)]
    reduce_sum x8 -> x1, other arithmetic: 7.9 us -> 0.78 us  [per_device(): totals = jnp.sum(stats[:, 0, :], axis=0)[:ns * MAXLEN].reshape(ns, MAXLEN)]
  transfers between devices with their start and end apart: 10 -> 0, of which waited for: 9 -> 0; matrix products, arithmetic and copies ran while one was open for 4% -> 0% of each run, Pallas kernels for 0% -> 0%
where the time goes in v1:
time: 275 us
  Pallas kernels  213 us (77%)
  blocking collectives  43.3 us (16%)
  local copies, waits for them, and re-layouts  7.28 us (3%)
  matrix products  5.68 us (2%)
  other arithmetic  4.81 us (2%)
    pallas_call x1, Pallas kernels, per_device(): pl.pallas_call(functools.partial(window_kernel, n, ns, ring), out_shape=(...  213 us
    all_gather x1, blocking collectives, per_device(): table = lax.all_gather(packed, ('group', 'section'), axis=0, tiled=True)  43.3 us
    dot_general x1, matrix products, per_device(): jnp.dot(choosing, unembed, preferred_element_type=jnp.float32)  5.68 us

profile of v1, /device:TPU:0, one launch (start us, length us, event | category | flops | bytes accessed | tf_op | source)
XLA Modules:
  0.0 275.1 jit_solution(4705302248341043936)
XLA Ops:
  0.7 0.8 copy.28
  1.4 0.1 reshape.102
  1.5 0.8 add_bitcast_fusion
  2.3 1.3 broadcast_in_dim.20.final_gain
  3.6 43.3 %all-gather = s32[32,1,21]{2,1,0:T(1,128)S(1)} all-gather(s32[1,1,21]{2,1,0:T(1,128)S(1)} %add_bitcast_fusion), channel_id=1, replica_groups=mesh['group'=8,'section'=4] {'group','section'}, dimensions={0}, use_global_device_ids=true | all-gather | bytes 2772 | tf_op jit(solution)/shard_map/all_gather | solution.py:428
  46.9 0.1 slice_compare_fusion
  46.9 0.2 reduce_window_sum.11
  47.1 0.1 copy.29
  47.2 0.1 convert_reduce_fusion
  47.3 0.1 broadcast_add_fusion
  47.4 0.1 add.72
  47.5 0.2 add_add_fusion
  47.7 0.1 eq.127
  47.7 0.1 fusion.9
  47.8 0.1 eq.131
  47.9 0.1 copy.30
  48.0 0.1 select_reduce_fusion
  48.1 0.1 convert_element_type.45
  48.2 0.7 fusion.10
  48.9 0.1 slice.48
  49.0 0.1 reshape.103
  49.0 0.2 slice_reduce_fusion.1
  49.2 0.7 reshape.110.hit
  50.0 0.7 fusion.6.mask
  50.7 0.3 fusion.7
  51.0 0.8 pad_maximum_fusion
  51.7 5.7 %convolution_convert_fusion = bf16[128,1792]{1,0:T(8,128)(2,1)} fusion(bf16[2432,1792]{1,0:T(8,128)(2,1)} %param.29, s32[2432]{0:T(1024)S(1)} %iota_add_fusion, s32[128]{0:T(128)S(1)} %get-tuple-element.8, s32[128]{0:T(128)S(1)} %get-tuple-element.7), kind=kOutput, calls=%fused_computation | convolution fusion | flops 1117470720 | bytes 9185792 | tf_op jit(solution)/shard_map/dot_general | solution.py:440
  57.4 213.3 %shard_map.166 = (bf16[32,1792]{1,0:T(8,128)(2,1)}, f32[8,24,128]{2,1,0:T(8,128)}) custom-call(bf16[32,1792]{1,0:T(8,128)(2,1)} %bitcast.21, bf16[224,1792]{1,0:T(8,128)(2,1)} %bitcast.15, bf16[224,512]{1,0:T(8,128)(2,1)} %bitcast.19, bf16[224,1792]{1,0:T(8,128)(2,1)} %bitcast.16, bf16[8,16,1792]{2,1,0:T(8,128)(2,1)} %bitcast.18, ...), custom_call_target="tpu_custom_call" | custom-call | tf_op jit(solution)/shard_map/pallas_call | solution.py:480
  270.8 1.3 dynamic-slice_reduce_fusion
  272.1 0.8 slice_reduce_fusion.2
  272.9 0.7 reshape.105
  273.5 1.6 copy.33
  (8 shorter events, 0.0 us)

commit v2 on v1

--- a/solution.py
+++ b/solution.py
@@ -21,6 +21,70 @@
     x = rows.astype(jnp.float32)
     scaled = x * lax.rsqrt(jnp.mean(x * x, axis=-1, keepdims=True) + EPS)
     return (scaled * gain).astype(jnp.bfloat16)
+
+
+def share_kernel(n, ns, tile, out, send, recv, local):
+    g = lax.axis_index("group")
+    s = lax.axis_index("section")
+    total = n * ns
+    me = g * ns + s
+    greet_all(me, ns, total)
+
+    def copy(i, slot):
+        t = lax.rem(me + i, total)
+        return pltpu.make_async_remote_copy(
+            src_ref=tile,
+            dst_ref=out.at[slot],
+            send_sem=send.at[i],
+            recv_sem=recv.at[slot],
+            device_id=(t // ns, lax.rem(t, ns)),
+            device_id_type=MESH,
+        )
+
+    def start(i, c):
+        copy(i, me).start()
+        return c
+
+    def finish(i, c):
+        copy(i, lax.rem(me + i, total)).wait_recv()
+        return c
+
+    def sent(i, c):
+        copy(i, me).wait_send()
+        return c
+
+    lax.fori_loop(1, total, start, 0)
+    own = pltpu.make_async_copy(tile, out.at[me], local)
+    own.start()
+    lax.fori_loop(1, total, finish, 0)
+    lax.fori_loop(1, total, sent, 0)
+    own.wait()
+
+
+def share(packed, n, ns):
+    total = n * ns
+    vmem = pl.BlockSpec(memory_space=pltpu.VMEM)
+    dma = pltpu.SemaphoreType.DMA
+    return pl.pallas_call(
+        functools.partial(share_kernel, n, ns),
+        out_shape=jax.ShapeDtypeStruct((total,) + packed.shape, packed.dtype),
+        in_specs=[vmem],
+        out_specs=vmem,
+        scratch_shapes=[dma((total,)), dma((total,)), dma],
+        compiler_params=pltpu.CompilerParams(collective_id=1, has_side_effects=True),
+    )(packed)
+
+
+def greet_all(me, ns, total):
+    barrier = pltpu.get_barrier_semaphore()
+
+    def greet(i, c):
+        t = lax.rem(me + i, total)
+        pl.semaphore_signal(barrier, inc=1, device_id=(t // ns, lax.rem(t, ns)), device_id_type=MESH)
+        return c
+
+    lax.fori_loop(1, total, greet, 0)
+    pl.semaphore_wait(barrier, total - 1)
 
 
 def ring_group(place, n):
@@ -36,7 +100,8 @@
     wq,
     wkv,
     wo,
-    terms,
+    unembed,
+    choose,
     clean,
     hit,
     mask,
@@ -50,7 +115,8 @@
     pick,
     cells,
     rows_out,
-    stats_out,
+    totals_out,
+    diffs_out,
     wq_all,
     wkv_all,
     wo_all,
@@ -63,6 +129,10 @@
     att,
     term_buf,
     stat,
+    stats_all,
+    shard_rows,
+    terms,
+    u_sem,
     w_send,
     w_recv,
     w_local,
@@ -91,15 +161,9 @@
     heads = width // HD
     per = heads // kv_heads
 
-    barrier = pltpu.get_barrier_semaphore()
-
-    def greet(i, c):
-        t = lax.rem(me + i, total)
-        pl.semaphore_signal(barrier, inc=1, device_id=(t // ns, lax.rem(t, ns)), device_id_type=MESH)
-        return c
-
-    lax.fori_loop(1, total, greet, 0)
-    pl.semaphore_wait(barrier, total - 1)
+    greet_all(me, ns, total)
+    vocab = pltpu.make_async_copy(unembed, shard_rows, u_sem)
+    vocab.start()
 
     ins = (wq, wkv, wo)
     alls = (wq_all, wkv_all, wo_all)
@@ -163,6 +227,19 @@
     @pl.when(s == 0)
     def _():
         e_own.start()
+
+    vocab.wait()
+    block = terms.shape[1]
+
+    def term_tile(t, c):
+        cols = pl.ds(pl.multiple_of(t * TILE, TILE), TILE)
+        part = jnp.dot(choose[...], shard_rows[:, cols], preferred_element_type=jnp.float32)
+        part = part.astype(jnp.bfloat16)
+        for k in range(n):
+            terms[k, :, cols] = part[k * block : (k + 1) * block]
+        return c
+
+    lax.fori_loop(0, d // TILE, term_tile, 0)
 
     def term_copy(i, slot):
         t = lax.rem(g + i, n)
@@ -300,7 +377,7 @@
         t = lax.rem(me + i, total)
         return pltpu.make_async_remote_copy(
             src_ref=stat,
-            dst_ref=stats_out.at[slot],
+            dst_ref=stats_all.at[slot],
             send_sem=s_send.at[i],
             recv_sem=s_recv.at[slot],
             device_id=(t // ns, lax.rem(t, ns)),
@@ -338,7 +415,7 @@
         stat[:STAT, :] = jnp.broadcast_to(
             jnp.sum(diffs * cells[...], axis=0, keepdims=True), (STAT, HD)
         )
-        s_own = pltpu.make_async_copy(stat, stats_out.at[g], s_send.at[0])
+        s_own = pltpu.make_async_copy(stat, stats_all.at[g], s_send.at[0])
         s_own.start()
 
         def send_stat(i, c):
@@ -380,6 +457,17 @@
         return c
 
     lax.fori_loop(1, n, term_sent, 0)
+    summed = stats_all[0, :STAT, :]
+    for k in range(1, n):
+        summed = summed + stats_all[k, :STAT, :]
+    totals_out[...] = summed
+    prompts = diffs_out.shape[0]
+    mine = stats_all[g]
+    for k in range(ns):
+
+        @pl.when(s == k)
+        def _():
+            diffs_out[...] = mine[STAT + k * prompts : STAT + (k + 1) * prompts]
 
 
 def bucket_layout(lengths_rows, seq_len):
@@ -425,7 +513,8 @@
     packed = jnp.concatenate(
         [lengths, patch_layer, patch_pos, answers.reshape(1, 2 * prompts)], axis=1
     )
-    table = lax.all_gather(packed, ("group", "section"), axis=0, tiled=True)
+    tile = jnp.pad(packed, ((0, 7), (0, HD - packed.shape[1])))
+    table = share(tile, n, ns)[:, 0, : packed.shape[1]]
     at = entries + 2 * prompts
     answer_ids = table[:, at:].reshape(total * prompts, 2)
     mine = lax.dynamic_slice_in_dim(table, g * ns, ns, 0)
@@ -437,9 +526,6 @@
     choosing = (answer_ids[:, 0:1] == vocab_ids[None, :]).astype(jnp.bfloat16) - (
         answer_ids[:, 1:2] == vocab_ids[None, :]
     ).astype(jnp.bfloat16)
-    terms = jnp.dot(choosing, unembed, preferred_element_type=jnp.float32).astype(jnp.bfloat16)
-    terms = terms.reshape(n, ns * prompts, d)
-
     segment, position, starts = bucket_layout(lens, seq_len)
     row_ids = jnp.arange(seq_len, dtype=jnp.int32)
     folded = offsets % lens[:, :prompts]
@@ -477,14 +563,15 @@
     vmem = pl.BlockSpec(memory_space=pltpu.VMEM)
     dma = pltpu.SemaphoreType.DMA
     stat_rows = STAT + ns * prompts
-    rows, stats = pl.pallas_call(
+    rows, totals, diffs = pl.pallas_call(
         functools.partial(window_kernel, n, ns, ring),
         out_shape=(
             jax.ShapeDtypeStruct((seq_len, d), jnp.bfloat16),
-            jax.ShapeDtypeStruct((n, stat_rows, HD), jnp.float32),
+            jax.ShapeDtypeStruct((STAT, HD), jnp.float32),
+            jax.ShapeDtypeStruct((prompts, HD), jnp.float32),
         ),
-        in_specs=[any_] * 5 + [vmem] * 12,
-        out_specs=(vmem, vmem),
+        in_specs=[any_] * 5 + [vmem] * 13,
+        out_specs=(vmem, vmem, vmem),
         scratch_shapes=[
             pltpu.VMEM((d, width), jnp.bfloat16),
             pltpu.VMEM((d, 2 * kvw), jnp.bfloat16),
@@ -498,6 +585,10 @@
             pltpu.VMEM((rows_all, width), jnp.bfloat16),
             pltpu.VMEM((total, ns * prompts, d), jnp.bfloat16),
             pltpu.VMEM((stat_rows, HD), jnp.float32),
+            pltpu.VMEM((n, stat_rows, HD), jnp.float32),
+            pltpu.VMEM(unembed.shape, jnp.bfloat16),
+            pltpu.VMEM((n, ns * prompts, d), jnp.bfloat16),
+            dma,
             dma((2, hops, 3)),
             dma((2, hops, 3)),
             dma((3,)),
@@ -521,7 +612,8 @@
         wq,
         wkv,
         wo,
-        terms,
+        unembed,
+        choosing,
         clean_cache[0].reshape(rows_all, d),
         hit,
         mask,
@@ -535,10 +627,8 @@
         pick,
         cells,
     )
-    totals = jnp.sum(stats[:, 0, :], axis=0)[: ns * MAXLEN].reshape(ns, MAXLEN)
-    group_diffs = lax.dynamic_slice_in_dim(stats, g, 1, 0)[0, STAT:, 0]
-    diffs = lax.dynamic_slice_in_dim(group_diffs, s * prompts, prompts, 0)
-    return (rows[None], diffs[None, :], totals)
+    totals = totals[0, : ns * MAXLEN].reshape(ns, MAXLEN)
+    return (rows[None], diffs[:, 0][None, :], totals)
 
 
 def solution(mesh):

time: 275 us -> 244 us (0.89)
  blocking collectives: 43.3 us -> 0 us
  Pallas kernels: 213 us -> 229 us
  matrix products: 5.68 us -> 0 us
    all_gather x1 -> x0, blocking collectives: 43.3 us -> none  [per_device(): table = lax.all_gather(packed, ('group', 'section'), axis=0, tiled=True)]
    pallas_call x0 -> x1, Pallas kernels: none -> 12.1 us  [share(): pl.pallas_call(functools.partial(share_kernel, n, ns), out_shape=jax.Shap...]
    dot_general x1 -> x0, matrix products: 5.68 us -> none  [per_device(): jnp.dot(choosing, unembed, preferred_element_type=jnp.float32)]
    pallas_call x1, Pallas kernels: 213 us -> 216 us  [per_device(): pl.pallas_call(functools.partial(window_kernel, n, ns, ring), out_shape=(...]
    slice x0 -> x3, local copies, waits for them, and re-layouts: none -> 2.91 us  [the longest x1 1.3 us: per_device(): return (rows[None], diffs[:, 0][None, :], totals)]
where the time goes in v2:
time: 244 us
  Pallas kernels  229 us (94%)
  local copies, waits for them, and re-layouts  9.47 us (4%)
  other arithmetic  5.16 us (2%)
    pallas_call x1, Pallas kernels, per_device(): pl.pallas_call(functools.partial(window_kernel, n, ns, ring), out_shape=(...  216 us
    pallas_call x1, Pallas kernels, share(): pl.pallas_call(functools.partial(share_kernel, n, ns), out_shape=jax.Shap...  12.1 us

profile of v2, /device:TPU:0, one launch (start us, length us, event | category | flops | bytes accessed | tf_op | source)
XLA Modules:
  0.0 243.9 jit_solution(8894797916426435602)
XLA Ops:
  0.7 0.8 copy.26
  1.4 0.1 reshape.95
  1.5 0.8 pad_add_fusion
  2.3 0.6 pad.4.tile
  2.9 1.3 broadcast_in_dim.18.final_gain
  4.2 12.1 %shard_map.166 = s32[32,8,128]{2,1,0:T(8,128)} custom-call(s32[8,128]{1,0:T(8,128)} %pad.4.tile), custom_call_target="tpu_custom_call" | custom-call | tf_op jit(solution)/shard_map/pallas_call | solution.py:68
  16.3 0.9 slice.37
  17.2 0.1 slice_compare_fusion
  17.3 0.2 reduce_window_sum.11
  17.5 0.1 copy.27
  17.6 0.1 convert_reduce_fusion
  17.7 0.1 add.68
  17.8 0.2 add_add_fusion
  18.0 0.1 eq.127
  18.1 0.1 fusion.5
  18.2 0.1 eq.131
  18.3 0.1 copy.28
  18.4 0.1 select_reduce_fusion
  18.5 0.1 convert_element_type.41
  18.5 0.7 fusion.6
  19.3 0.1 reshape.96
  19.4 0.2 slice_reduce_fusion.1
  19.6 0.7 reshape.98.hit
  20.3 0.7 fusion.2.mask
  21.0 0.3 fusion.3
  21.3 0.8 pad_maximum_fusion
  22.1 1.1 fusion.choose
  23.2 216.4 %shard_map.167 = (bf16[32,1792]{1,0:T(8,128)(2,1)}, f32[8,128]{1,0:T(8,128)}, f32[4,128]{1,0:T(4,128)}) custom-call(bf16[32,1792]{1,0:T(8,128)(2,1)} %bitcast.14, bf16[224,1792]{1,0:T(8,128)(2,1)} %bitcast.10, bf16[224,512]{1,0:T(8,128)(2,1)} %bitcast.13, bf16[224,1792]{1,0:T(8,128)(2,1)} %bitcast.11, bf16[2432,1792]{1,0:T(8,128)(2,1)} %unembed.1, ...), custom_call_target="tpu_custom_call" | custom-call | tf_op jit(solution)/shard_map/pallas_call | solution.py:566
  239.7 1.3 slice_reduce_fusion.2
  241.0 0.7 slice_reduce_fusion.3
  241.7 0.7 reshape_squeeze.7
  242.3 1.6 copy.31
  (10 shorter events, 0.2 us)

commit v3 on v2

--- a/solution.py
+++ b/solution.py
@@ -87,30 +87,42 @@
     pl.semaphore_wait(barrier, total - 1)
 
 
-def ring_group(place, n):
-    late = place // (n // 2)
-    return (1 - late) * 2 * place + late * (2 * (n - 1 - place) + 1)
+def sliced(n, ns, shard):
+    return ns == 4 and n == 2 * ns and shard % 32 == 0
+
+
+def worker(layer, q, n, ns, by_slice):
+    if by_slice:
+        return layer * (n // ns) + q // ns, lax.rem(q, ns)
+    return q, layer
+
+
+def role(n, ns, by_slice):
+    g = lax.axis_index("group")
+    s = lax.axis_index("section")
+    if by_slice:
+        m = n // ns
+        return g // m, lax.rem(g, m) * ns + s
+    return s, g
 
 
 def window_kernel(
     n,
     ns,
-    ring,
+    by_slice,
     embed,
     wq,
     wkv,
     wo,
     unembed,
+    params,
+    clean,
     choose,
-    clean,
-    hit,
+    patch_pick,
+    place,
     mask,
     cosine,
     sinus,
-    gain,
-    bq,
-    bk,
-    bv,
     final_gain,
     pick,
     cells,
@@ -132,15 +144,20 @@
     stats_all,
     shard_rows,
     terms,
+    patches,
+    patch_rows,
+    layer_params,
     u_sem,
     w_send,
     w_recv,
     w_local,
+    f_send,
     e_send,
     e_recv,
+    c_send,
+    c_recv,
     t_send,
     t_recv,
-    t_local,
     h_send,
     h_recv,
     r_send,
@@ -153,6 +170,7 @@
     total = n * ns
     me = g * ns + s
     last = ns - 1
+    layer, q = role(n, ns, by_slice)
     bucket = embed.shape[0]
     d = embed.shape[1]
     width = wq_all.shape[1]
@@ -161,6 +179,24 @@
     heads = width // HD
     per = heads // kv_heads
 
+    def serves(which, group):
+        a, b = worker(which, group, n, ns, by_slice)
+        return a * ns + b
+
+    def send(src, dst, send_sem, recv_sem, target):
+        return pltpu.make_async_remote_copy(
+            src_ref=src,
+            dst_ref=dst,
+            send_sem=send_sem,
+            recv_sem=recv_sem,
+            device_id=(target // ns, lax.rem(target, ns)),
+            device_id_type=MESH,
+        )
+
+    def either(target, remote, local):
+        pl.when(target != me)(remote)
+        pl.when(target == me)(local)
+
     greet_all(me, ns, total)
     vocab = pltpu.make_async_copy(unembed, shard_rows, u_sem)
     vocab.start()
@@ -168,65 +204,74 @@
     ins = (wq, wkv, wo)
     alls = (wq_all, wkv_all, wo_all)
     shard = wq.shape[0]
-    if ring:
-        odd = lax.rem(g, 2)
-        place = (1 - odd) * (g // 2) + odd * (n - 1 - g // 2)
-        right = ring_group(lax.rem(place + 1, n), n)
-        left = ring_group(lax.rem(place + n - 1, n), n)
-        half = n // 2
-
-        def rows_of(step, way):
-            at = lax.rem(place + n - step, n) if way == 0 else lax.rem(place + step, n)
-            return pl.ds(pl.multiple_of(ring_group(at, n) * shard, shard), shard)
-
-        def hop(step, way, a):
-            rows = rows_of(step, way)
-            src = ins[a] if step == 0 else alls[a].at[rows]
-            return pltpu.make_async_remote_copy(
-                src_ref=src,
-                dst_ref=alls[a].at[rows],
-                send_sem=w_send.at[way, step, a],
-                recv_sem=w_recv.at[way, step, a],
-                device_id=((right, left)[way], s),
-                device_id_type=MESH,
+    if by_slice:
+        part = shard // 2
+        chunks = [(0, 0, part), (0, part, part), (1, 0, shard), (2, 0, part), (2, part, part)]
+        y = lax.rem(g, 2)
+        z = g // 2
+        x = s // 2
+        c = lax.rem(s, 2)
+
+        def span(ch, origin):
+            a, first, count = chunks[ch]
+            return alls[a].at[pl.ds(pl.multiple_of(origin * shard + first, 16), count)]
+
+        def fresh(ch):
+            a, first, count = chunks[ch]
+            return ins[a].at[pl.ds(first, count)]
+
+        entry = (s * 2 + y) * ns + x * 2 + lax.rem(z, 2)
+
+        def outward(ch):
+            return send(fresh(ch), span(ch, g), w_send.at[ch], w_recv.at[g, ch], entry)
+
+        def homeward(ch):
+            return pltpu.make_async_copy(fresh(ch), span(ch, g), w_local.at[ch])
+
+        @pl.when(z != s)
+        def _():
+            for ch in range(len(chunks)):
+                outward(ch).start()
+
+        @pl.when(z == s)
+        def _():
+            for ch in range(len(chunks)):
+                homeward(ch).start()
+
+        side = z // 2
+        near = c + 2 * side
+        far = c + 2 * (1 - side)
+        routes = ((near, y), (far, y), (near, 1 - y), (far, 1 - y))
+
+        def onward(ch, k, way):
+            zz, yy = routes[k]
+            origin = zz * 2 + yy
+            target = (
+                g * ns + x * 2 + 1 - c,
+                (z * 2 + 1 - y) * ns + s,
+                g * ns + (1 - x) * 2 + c,
+            )[way]
+            return send(
+                span(ch, origin), span(ch, origin), f_send.at[k, way, ch], w_recv.at[origin, ch], target
             )
 
-        def used(step, way, a):
-            if step < half - 1:
-                return True
-            return (a == 0) if way == 0 else (a != 0)
-
-        for a in range(3):
-            for way in range(2):
-                if used(0, way, a):
-                    hop(0, way, a).start()
-        own = pl.ds(pl.multiple_of(g * shard, shard), shard)
     else:
-        own = pl.ds(0, shard)
-    local = [
-        pltpu.make_async_copy(ins[a], alls[a].at[own], w_local.at[a]) for a in range(3)
-    ]
-    for copy in local:
-        copy.start()
+        local = [pltpu.make_async_copy(ins[a], alls[a], w_local.at[a]) for a in range(3)]
+        for copy in local:
+            copy.start()
 
     own_rows = pl.ds(pl.multiple_of(s * bucket, bucket), bucket)
-    e_out = pltpu.make_async_remote_copy(
-        src_ref=embed,
-        dst_ref=h_in.at[own_rows],
-        send_sem=e_send,
-        recv_sem=e_recv.at[s],
-        device_id=(g, 0),
-        device_id_type=MESH,
-    )
+    first = serves(0, g)
+    e_out = send(embed, h_in.at[own_rows], e_send, e_recv.at[s], first)
     e_own = pltpu.make_async_copy(embed, h_in.at[own_rows], e_send)
-
-    @pl.when(s != 0)
-    def _():
-        e_out.start()
-
-    @pl.when(s == 0)
-    def _():
-        e_own.start()
+    either(first, e_out.start, e_own.start)
+    user = serves(s, g)
+    p_out = send(params, layer_params, c_send.at[0], c_recv.at[0], user)
+    p_own = pltpu.make_async_copy(params, layer_params, c_send.at[0])
+    either(user, p_out.start, p_own.start)
+    patches[...] = jnp.dot(
+        patch_pick[...], clean[...], preferred_element_type=jnp.float32
+    ).astype(jnp.bfloat16)
 
     vocab.wait()
     block = terms.shape[1]
@@ -241,92 +286,113 @@
 
     lax.fori_loop(0, d // TILE, term_tile, 0)
 
-    def term_copy(i, slot):
-        t = lax.rem(g + i, n)
-        return pltpu.make_async_remote_copy(
-            src_ref=terms.at[t],
-            dst_ref=term_buf.at[slot],
-            send_sem=t_send.at[i],
-            recv_sem=t_recv.at[slot],
-            device_id=(t, last),
-            device_id_type=MESH,
+    def term_copy(t, slot):
+        return send(
+            terms.at[t], term_buf.at[slot], t_send.at[t], t_recv.at[slot], serves(last, t)
         )
 
-    def send_term(i, c):
-        term_copy(i, me).start()
-        return c
-
-    t_own = pltpu.make_async_copy(terms.at[g], term_buf.at[me], t_local)
-
-    @pl.when(s == last)
+    def term_own(t):
+        return pltpu.make_async_copy(terms.at[t], term_buf.at[me], t_send.at[t])
+
+    def send_term(t, c):
+        either(
+            serves(last, t),
+            lambda: term_copy(t, me).start(),
+            lambda: term_own(t).start(),
+        )
+        return c
+
+    lax.fori_loop(0, n, send_term, 0)
+    c_out = send(patches, patch_rows, c_send.at[1], c_recv.at[1], user)
+    c_own = pltpu.make_async_copy(patches, patch_rows, c_send.at[1])
+    either(user, c_out.start, c_own.start)
+
+    if by_slice:
+        for ch in range(len(chunks)):
+            for k in range(4):
+                if k == 0:
+
+                    @pl.when(z == s)
+                    def _():
+                        homeward(ch).wait()
+
+                    @pl.when(z != s)
+                    def _():
+                        onward(ch, 0, 0).wait_recv()
+
+                else:
+                    onward(ch, k, 0).wait_recv()
+                if k < 2:
+                    onward(ch, k, 1).start()
+
+                    @pl.when(x == side)
+                    def _():
+                        onward(ch, k, 2).start()
+
+                onward(ch, k, 0).start()
+        for ch in range(len(chunks)):
+            for zz in (1 - c, 3 - c):
+                for yy in range(2):
+                    origin = zz * 2 + yy
+                    send(
+                        span(ch, origin), span(ch, origin), w_send.at[ch], w_recv.at[origin, ch], entry
+                    ).wait_recv()
+    else:
+        for copy in local:
+            copy.wait()
+
+    tiles = d // TILE
+
+    def h_copy(t):
+        cols = pl.ds(pl.multiple_of(t * TILE, TILE), TILE)
+        target = serves(lax.rem(layer + 1, ns), q)
+        return send(h_out.at[:, cols], h_in.at[:, cols], h_send.at[t], h_recv.at[t], target)
+
+    either(first, lambda: None, e_own.wait)
+
+    @pl.when(layer == 0)
     def _():
-        t_own.start()
-
-    @pl.when(s != last)
+        for i in range(ns):
+
+            @pl.when(q * ns + i != me)
+            def _():
+                rows = pl.ds(i * bucket, bucket)
+                send(embed, h_in.at[rows], e_send, e_recv.at[i], first).wait_recv()
+
+    source = q * ns + layer
+
+    @pl.when(source != me)
     def _():
-        term_copy(0, me).start()
-
-    lax.fori_loop(1, n, send_term, 0)
-
-    if ring:
-        for step in range(1, half):
-            for a in range(3):
-                for way in range(2):
-                    hop(step - 1, way, a).wait_recv()
-                    if used(step, way, a):
-                        hop(step, way, a).start()
-        for a in range(3):
-            for way in range(2):
-                if used(half - 1, way, a):
-                    hop(half - 1, way, a).wait_recv()
-        for step in range(half):
-            for a in range(3):
-                for way in range(2):
-                    if used(step, way, a):
-                        hop(step, way, a).wait_send()
-    for copy in local:
-        copy.wait()
-
-    h_copy = pltpu.make_async_remote_copy(
-        src_ref=h_out,
-        dst_ref=h_in,
-        send_sem=h_send,
-        recv_sem=h_recv,
-        device_id=(g, lax.rem(s + 1, ns)),
-        device_id_type=MESH,
-    )
-
-    @pl.when(s == 0)
+        p_out.wait_recv()
+        c_out.wait_recv()
+
+    either(user, lambda: None, p_own.wait)
+    either(user, lambda: None, c_own.wait)
+
+    @pl.when(layer != 0)
     def _():
-        e_own.wait()
-        for i in range(1, ns):
-            rows = pl.ds(i * bucket, bucket)
-            pltpu.make_async_remote_copy(
-                src_ref=embed,
-                dst_ref=h_in.at[rows],
-                send_sem=e_send,
-                recv_sem=e_recv.at[i],
-                device_id=(g, 0),
-                device_id_type=MESH,
-            ).wait_recv()
-
-    @pl.when(s != 0)
-    def _():
-        e_out.wait_send()
-        h_copy.wait_recv()
-
-    h_in[...] = jnp.where(hit[...] > 0, clean[...], h_in[...])
-    normed[...] = rms(h_in[...], gain[...])
+        for t in range(tiles):
+            h_copy(t).wait_recv()
+
+    gain = layer_params[:, :d]
+    bq = layer_params.at[:, pl.ds(d, width)]
+    bk = layer_params[:, d + width : d + width + kvw]
+    bv = layer_params[:, d + width + kvw :]
+
+    fill = jnp.dot(place[...], patch_rows[...], preferred_element_type=jnp.float32)
+    hit = jnp.sum(place[...].astype(jnp.float32), axis=-1, keepdims=True) > 0
+    h_in[...] = jnp.where(hit, fill, h_in[...].astype(jnp.float32)).astype(jnp.bfloat16)
+    normed[...] = rms(h_in[...], gain)
     cos_t = cosine[...]
     sin_t = sinus[...]
 
     def rotate(x):
         return (x * cos_t + pltpu.roll(x, HD // 2, 1) * sin_t).astype(jnp.bfloat16)
 
-    keys = jnp.dot(normed[...], wkv_all[:, :kvw], preferred_element_type=jnp.float32) + bk[...]
+    keys = jnp.dot(normed[...], wkv_all[:, :kvw], preferred_element_type=jnp.float32) + bk
     for k in range(kv_heads):
         k_rot[k] = rotate(keys[:, k * HD : (k + 1) * HD])
-    values = jnp.dot(normed[...], wkv_all[:, kvw:], preferred_element_type=jnp.float32) + bv[...]
+    values = jnp.dot(normed[...], wkv_all[:, kvw:], preferred_element_type=jnp.float32) + bv
     v_all[...] = values.astype(jnp.bfloat16)
 
     def query_tile(t, c):
@@ -355,22 +421,27 @@
         cols = pl.ds(pl.multiple_of(t * TILE, TILE), TILE)
         up = jnp.dot(att[...], wo_all[:, cols], preferred_element_type=jnp.float32)
         h_out[:, cols] = (h_in[:, cols].astype(jnp.float32) + up).astype(jnp.bfloat16)
-        return c
-
-    lax.fori_loop(0, d // TILE, out_tile, 0)
-
-    @pl.when(s != last)
+
+        @pl.when((t > 0) & (layer != last))
+        def _():
+            h_copy(t - 1).start()
+
+        return c
+
+    lax.fori_loop(0, tiles, out_tile, 0)
+
+    @pl.when(layer != last)
     def _():
-        h_copy.start()
+        h_copy(tiles - 1).start()
 
     def row_copy(i):
-        return pltpu.make_async_remote_copy(
-            src_ref=h_out.at[pl.ds(i * bucket, bucket)],
-            dst_ref=rows_out,
-            send_sem=r_send.at[i],
-            recv_sem=r_recv,
-            device_id=(g, i),
-            device_id_type=MESH,
+        return send(
+            h_out.at[pl.ds(i * bucket, bucket)], rows_out, r_send.at[i], r_recv, q * ns + i
+        )
+
+    def row_own(i):
+        return pltpu.make_async_copy(
+            h_out.at[pl.ds(i * bucket, bucket)], rows_out, r_send.at[i]
         )
 
     def stat_copy(i, slot):
@@ -387,19 +458,14 @@
     def wait_stat(slot):
         stat_copy(1, slot).wait_recv()
 
-    @pl.when(s == last)
+    @pl.when(layer == last)
     def _():
-        for i in range(last):
-            row_copy(i).start()
-        row_own = pltpu.make_async_copy(
-            h_out.at[pl.ds(last * bucket, bucket)], rows_out, r_send.at[last]
-        )
-        row_own.start()
-
-        t_own.wait()
+        for i in range(ns):
+            either(q * ns + i, row_copy(i).start, row_own(i).start)
+        term_own(q).wait()
 
         def take_term(i, c):
-            term_copy(1, lax.rem(me + i, total)).wait_recv()
+            term_copy(q, lax.rem(me + i, total)).wait_recv()
             return c
 
         lax.fori_loop(1, total, take_term, 0)
@@ -415,36 +481,34 @@
         stat[:STAT, :] = jnp.broadcast_to(
             jnp.sum(diffs * cells[...], axis=0, keepdims=True), (STAT, HD)
         )
-        s_own = pltpu.make_async_copy(stat, stats_all.at[g], s_send.at[0])
+        s_own = pltpu.make_async_copy(stat, stats_all.at[q], s_send.at[0])
         s_own.start()
 
         def send_stat(i, c):
-            stat_copy(i, g).start()
+            stat_copy(i, q).start()
             return c
 
         lax.fori_loop(1, total, send_stat, 0)
 
         def others(i, c):
-            wait_stat(lax.rem(g + i, n))
+            wait_stat(lax.rem(q + i, n))
             return c
 
         lax.fori_loop(1, n, others, 0)
 
         def sent(i, c):
-            stat_copy(i, g).wait_send()
+            stat_copy(i, q).wait_send()
             return c
 
         lax.fori_loop(1, total, sent, 0)
         s_own.wait()
-        row_own.wait()
-        for i in range(last):
-            row_copy(i).wait_send()
-
-    @pl.when(s != last)
+        for i in range(ns):
+            either(q * ns + i, row_copy(i).wait_send, row_own(i).wait)
+
+    @pl.when(layer != last)
     def _():
-        h_copy.wait_send()
-        term_copy(0, me).wait_send()
-        row_copy(0).wait_recv()
+        for t in range(tiles):
+            h_copy(t).wait_send()
 
         def every(i, c):
             wait_stat(i)
@@ -452,11 +516,35 @@
 
         lax.fori_loop(0, n, every, 0)
 
-    def term_sent(i, c):
-        term_copy(i, me).wait_send()
-        return c
-
-    lax.fori_loop(1, n, term_sent, 0)
+    @pl.when(serves(last, g) != me)
+    def _():
+        row_copy(0).wait_recv()
+
+    def term_sent(t, c):
+        pl.when(serves(last, t) != me)(lambda: term_copy(t, me).wait_send())
+        return c
+
+    lax.fori_loop(0, n, term_sent, 0)
+    either(first, e_out.wait_send, lambda: None)
+    either(user, p_out.wait_send, lambda: None)
+    either(user, c_out.wait_send, lambda: None)
+    if by_slice:
+
+        @pl.when(z != s)
+        def _():
+            for ch in range(len(chunks)):
+                outward(ch).wait_send()
+
+        for ch in range(len(chunks)):
+            for k in range(4):
+                onward(ch, k, 0).wait_send()
+                if k < 2:
+                    onward(ch, k, 1).wait_send()
+
+                    @pl.when(x == side)
+                    def _():
+                        onward(ch, k, 2).wait_send()
+
     summed = stats_all[0, :STAT, :]
     for k in range(1, n):
         summed = summed + stats_all[k, :STAT, :]
@@ -517,11 +605,21 @@
     table = share(tile, n, ns)[:, 0, : packed.shape[1]]
     at = entries + 2 * prompts
     answer_ids = table[:, at:].reshape(total * prompts, 2)
-    mine = lax.dynamic_slice_in_dim(table, g * ns, ns, 0)
-    lens = mine[:, :entries]
-    layers = mine[:, entries : entries + prompts]
-    offsets = mine[:, entries + prompts : at]
-
+    by_slice = sliced(n, ns, w_query.shape[1])
+    layer, q = role(n, ns, by_slice)
+
+    def of_group(which):
+        part = lax.dynamic_slice_in_dim(table, which * ns, ns, 0)
+        return part[:, :entries], part[:, entries : entries + prompts], part[:, entries + prompts : at]
+
+    def targets(lens, offsets):
+        starts = jnp.cumsum(lens, axis=-1) - lens
+        folded = offsets % lens[:, :prompts]
+        base = jnp.arange(ns, dtype=jnp.int32)[:, None] * seq_len
+        return (starts[:, :prompts] + folded + base).reshape(-1)
+
+    lens_g, _, offsets_g = of_group(g)
+    lens, layers, offsets = of_group(q)
     vocab_ids = (g * ns + s) * unembed.shape[0] + jnp.arange(unembed.shape[0], dtype=jnp.int32)
     choosing = (answer_ids[:, 0:1] == vocab_ids[None, :]).astype(jnp.bfloat16) - (
         answer_ids[:, 1:2] == vocab_ids[None, :]
@@ -529,13 +627,13 @@
     segment, position, starts = bucket_layout(lens, seq_len)
     row_ids = jnp.arange(seq_len, dtype=jnp.int32)
     folded = offsets % lens[:, :prompts]
-    target = starts[:, :prompts] + folded
-    hit = jnp.any(
-        (row_ids[:, None] == target[:, None, :]) & (layers[:, None, :] == s), axis=-1
-    )
-    hit = hit.reshape(rows_all, 1).astype(jnp.float32)
+    all_rows = jnp.arange(rows_all, dtype=jnp.int32)
+    patch_pick = (targets(lens_g, offsets_g)[:, None] == all_rows[None, :]).astype(jnp.bfloat16)
+    place = (
+        (all_rows[:, None] == targets(lens, offsets)[None, :])
+        & (layers.reshape(1, -1) == layer)
+    ).astype(jnp.bfloat16)
     ident = (segment + jnp.arange(ns, dtype=jnp.int32)[:, None] * entries).reshape(rows_all)
-    all_rows = jnp.arange(rows_all, dtype=jnp.int32)
     mask = (
         (ident[:, None] == ident[None, :]) & (all_rows[None, :] <= all_rows[:, None])
     ).astype(jnp.float32)
@@ -555,22 +653,21 @@
     cells = (cell_ids[:, None] == jnp.arange(HD, dtype=jnp.int32)[None, :]).astype(jnp.float32)
 
     wq, wkv, wo = w_query[0], w_keyval[0], w_out[0]
-    ring = n % 2 == 0 and n > 2 and wq.shape[0] % 16 == 0
-    if not ring:
+    if not by_slice:
         wq, wkv, wo = (lax.all_gather(w, "group", axis=0, tiled=True) for w in (wq, wkv, wo))
-    hops = max(n // 2, 1) if ring else 1
+    params = jnp.concatenate([attn_gain, b_query, b_key, b_value], axis=1)
     any_ = pl.BlockSpec(memory_space=pl.ANY)
     vmem = pl.BlockSpec(memory_space=pltpu.VMEM)
     dma = pltpu.SemaphoreType.DMA
     stat_rows = STAT + ns * prompts
     rows, totals, diffs = pl.pallas_call(
-        functools.partial(window_kernel, n, ns, ring),
+        functools.partial(window_kernel, n, ns, by_slice),
         out_shape=(
             jax.ShapeDtypeStruct((seq_len, d), jnp.bfloat16),
             jax.ShapeDtypeStruct((STAT, HD), jnp.float32),
             jax.ShapeDtypeStruct((prompts, HD), jnp.float32),
         ),
-        in_specs=[any_] * 5 + [vmem] * 13,
+        in_specs=[any_] * 5 + [vmem] * 11,
         out_specs=(vmem, vmem, vmem),
         scratch_shapes=[
             pltpu.VMEM((d, width), jnp.bfloat16),
@@ -588,17 +685,22 @@
             pltpu.VMEM((n, stat_rows, HD), jnp.float32),
             pltpu.VMEM(unembed.shape, jnp.bfloat16),
             pltpu.VMEM((n, ns * prompts, d), jnp.bfloat16),
+            pltpu.VMEM((ns * prompts, d), jnp.bfloat16),
+            pltpu.VMEM((ns * prompts, d), jnp.bfloat16),
+            pltpu.VMEM(params.shape, jnp.float32),
             dma,
-            dma((2, hops, 3)),
-            dma((2, hops, 3)),
-            dma((3,)),
+            dma((5,)),
+            dma((n, 5)),
+            dma((5,)),
+            dma((4, 3, 5)),
             dma,
             dma((ns,)),
+            dma((2,)),
+            dma((2,)),
             dma((n,)),
             dma((total,)),
-            dma,
-            dma,
-            dma,
+            dma((d // TILE,)),
+            dma((d // TILE,)),
             dma((ns,)),
             dma,
             dma((total,)),
@@ -613,16 +715,14 @@
         wkv,
         wo,
         unembed,
+        params,
+        clean_cache[0].reshape(rows_all, d),
         choosing,
-        clean_cache[0].reshape(rows_all, d),
-        hit,
+        patch_pick,
+        place,
         mask,
         cosine,
         sinus,
-        attn_gain,
-        b_query,
-        b_key,
-        b_value,
         final_gain[None, :],
         pick,
         cells,

time: 244 us -> 244 us (level)
  Pallas kernels: 229 us -> 224 us
  other arithmetic: 5.16 us -> 9.22 us
    pallas_call x1, Pallas kernels: 216 us -> 212 us  [per_device(): pl.pallas_call(functools.partial(window_kernel, n, ns, by_slice), out_sha...]
where the time goes in v3:
time: 244 us; the launch traced here: 243 us
  Pallas kernels  224 us (92%)
  other arithmetic  9.22 us (4%)
  local copies, waits for them, and re-layouts  8.98 us (4%)
    pallas_call x1, Pallas kernels, per_device(): pl.pallas_call(functools.partial(window_kernel, n, ns, by_slice), out_sha...  212 us
    pallas_call x1, Pallas kernels, share(): pl.pallas_call(functools.partial(share_kernel, n, ns), out_shape=jax.Shap...  12.1 us

profile of v3, /device:TPU:0, one launch (start us, length us, event | category | flops | bytes accessed | tf_op | source)
XLA Modules:
  0.0 242.7 jit_solution(3216608097149486541)
XLA Ops:
  0.7 0.8 copy.26
  1.5 0.1 reshape.90
  1.5 0.8 pad_add_fusion
  2.3 0.6 pad.4.tile
  2.9 1.3 broadcast_in_dim.18.final_gain
  4.2 1.4 pad_maximum_fusion.2.params
  5.6 12.1 %shard_map.166 = s32[32,8,128]{2,1,0:T(8,128)} custom-call(s32[8,128]{1,0:T(8,128)} %pad.4.tile), custom_call_target="tpu_custom_call" | custom-call | tf_op jit(solution)/shard_map/pallas_call | solution.py:68
  17.6 0.9 slice.51
  18.7 0.1 eq.155
  18.7 0.2 reduce_window_sum.19
  18.9 0.2 reduce_window_sum.18
  19.1 0.2 add_add_fusion
  19.6 0.1 copy.29
  19.7 0.1 copy.28
  19.8 0.1 convert_reduce_fusion
  20.1 0.1 add.105
  20.2 0.1 convert_element_type.42
  20.2 0.7 fusion.6.patch_pick
  20.9 0.7 fusion.7.pick
  21.6 0.7 fusion.8.cells
  22.3 0.6 fusion.2.place
  23.0 0.2 slice_reduce_fusion.1
  23.2 0.7 fusion.4.mask
  23.9 0.3 fusion.5
  24.2 0.7 pad_maximum_fusion.1.sinus
  25.0 0.7 pad_maximum_fusion.cosine
  25.7 1.1 fusion.choose
  26.8 211.7 %shard_map.167 = (bf16[32,1792]{1,0:T(8,128)(2,1)}, f32[8,128]{1,0:T(8,128)}, f32[4,128]{1,0:T(4,128)}) custom-call(bf16[32,1792]{1,0:T(8,128)(2,1)} %bitcast.16, bf16[224,1792]{1,0:T(8,128)(2,1)} %bitcast.12, bf16[224,512]{1,0:T(8,128)(2,1)} %bitcast.15, bf16[224,1792]{1,0:T(8,128)(2,1)} %bitcast.13, bf16[2432,1792]{1,0:T(8,128)(2,1)} %unembed.1, ...), custom_call_target="tpu_custom_call" | custom-call | tf_op jit(solution)/shard_map/pallas_call | solution.py:663
  238.5 1.3 slice_reduce_fusion.2
  239.8 0.7 slice_reduce_fusion.3
  240.5 0.7 reshape_squeeze.7
  241.1 1.6 copy.31
  (16 shorter events, 0.7 us)

commit v4 on v2

--- a/solution.py
+++ b/solution.py
@@ -256,18 +256,6 @@
         term_copy(i, me).start()
         return c
 
-    t_own = pltpu.make_async_copy(terms.at[g], term_buf.at[me], t_local)
-
-    @pl.when(s == last)
-    def _():
-        t_own.start()
-
-    @pl.when(s != last)
-    def _():
-        term_copy(0, me).start()
-
-    lax.fori_loop(1, n, send_term, 0)
-
     if ring:
         for step in range(1, half):
             for a in range(3):
@@ -287,14 +275,30 @@
     for copy in local:
         copy.wait()
 
-    h_copy = pltpu.make_async_remote_copy(
-        src_ref=h_out,
-        dst_ref=h_in,
-        send_sem=h_send,
-        recv_sem=h_recv,
-        device_id=(g, lax.rem(s + 1, ns)),
-        device_id_type=MESH,
-    )
+    t_own = pltpu.make_async_copy(terms.at[g], term_buf.at[me], t_local)
+
+    @pl.when(s == last)
+    def _():
+        t_own.start()
+
+    @pl.when(s != last)
+    def _():
+        term_copy(0, me).start()
+
+    lax.fori_loop(1, n, send_term, 0)
+
+    tiles = d // TILE
+
+    def h_copy(t):
+        cols = pl.ds(pl.multiple_of(t * TILE, TILE), TILE)
+        return pltpu.make_async_remote_copy(
+            src_ref=h_out.at[:, cols],
+            dst_ref=h_in.at[:, cols],
+            send_sem=h_send.at[t],
+            recv_sem=h_recv.at[t],
+            device_id=(g, lax.rem(s + 1, ns)),
+            device_id_type=MESH,
+        )
 
     @pl.when(s == 0)
     def _():
@@ -313,7 +317,8 @@
     @pl.when(s != 0)
     def _():
         e_out.wait_send()
-        h_copy.wait_recv()
+        for t in range(tiles):
+            h_copy(t).wait_recv()
 
     h_in[...] = jnp.where(hit[...] > 0, clean[...], h_in[...])
     normed[...] = rms(h_in[...], gain[...])
@@ -355,13 +360,18 @@
         cols = pl.ds(pl.multiple_of(t * TILE, TILE), TILE)
         up = jnp.dot(att[...], wo_all[:, cols], preferred_element_type=jnp.float32)
         h_out[:, cols] = (h_in[:, cols].astype(jnp.float32) + up).astype(jnp.bfloat16)
-        return c
-
-    lax.fori_loop(0, d // TILE, out_tile, 0)
+
+        @pl.when((t > 0) & (s != last))
+        def _():
+            h_copy(t - 1).start()
+
+        return c
+
+    lax.fori_loop(0, tiles, out_tile, 0)
 
     @pl.when(s != last)
     def _():
-        h_copy.start()
+        h_copy(tiles - 1).start()
 
     def row_copy(i):
         return pltpu.make_async_remote_copy(
@@ -442,7 +452,8 @@
 
     @pl.when(s != last)
     def _():
-        h_copy.wait_send()
+        for t in range(tiles):
+            h_copy(t).wait_send()
         term_copy(0, me).wait_send()
         row_copy(0).wait_recv()
 
@@ -597,8 +608,8 @@
             dma((n,)),
             dma((total,)),
             dma,
-            dma,
-            dma,
+            dma((d // TILE,)),
+            dma((d // TILE,)),
             dma((ns,)),
             dma,
             dma((total,)),

time: 244 us -> 234 us (0.959)
  Pallas kernels: 229 us -> 219 us
    pallas_call x1, Pallas kernels: 216 us -> 207 us  [per_device(): pl.pallas_call(functools.partial(window_kernel, n, ns, ring), out_shape=(...]
where the time goes in v4:
time: 234 us
  Pallas kernels  219 us (94%)
  local copies, waits for them, and re-layouts  9.47 us (4%)
  other arithmetic  5.16 us (2%)
    pallas_call x1, Pallas kernels, per_device(): pl.pallas_call(functools.partial(window_kernel, n, ns, ring), out_shape=(...  207 us
    pallas_call x1, Pallas kernels, share(): pl.pallas_call(functools.partial(share_kernel, n, ns), out_shape=jax.Shap...  12.1 us

profile of v4, /device:TPU:0, one launch (start us, length us, event | category | flops | bytes accessed | tf_op | source)
XLA Modules:
  0.0 234.1 jit_solution(10971793283734964102)
XLA Ops:
  0.7 0.8 copy.26
  1.4 0.1 reshape.95
  1.5 0.8 pad_add_fusion
  2.3 0.6 pad.4.tile
  2.9 1.3 broadcast_in_dim.18.final_gain
  4.2 12.1 %shard_map.166 = s32[32,8,128]{2,1,0:T(8,128)} custom-call(s32[8,128]{1,0:T(8,128)} %pad.4.tile), custom_call_target="tpu_custom_call" | custom-call | tf_op jit(solution)/shard_map/pallas_call | solution.py:68
  16.3 0.9 slice.37
  17.2 0.1 slice_compare_fusion
  17.3 0.2 reduce_window_sum.11
  17.5 0.1 copy.27
  17.6 0.1 convert_reduce_fusion
  17.7 0.1 add.68
  17.8 0.2 add_add_fusion
  18.0 0.1 eq.127
  18.1 0.1 fusion.5
  18.2 0.1 eq.131
  18.3 0.1 copy.28
  18.4 0.1 select_reduce_fusion
  18.5 0.1 convert_element_type.41
  18.5 0.7 fusion.6
  19.3 0.1 reshape.96
  19.4 0.2 slice_reduce_fusion.1
  19.6 0.7 reshape.98.hit
  20.3 0.7 fusion.2.mask
  21.0 0.3 fusion.3
  21.3 0.8 pad_maximum_fusion
  22.1 1.1 fusion.choose
  23.2 206.7 %shard_map.167 = (bf16[32,1792]{1,0:T(8,128)(2,1)}, f32[8,128]{1,0:T(8,128)}, f32[4,128]{1,0:T(4,128)}) custom-call(bf16[32,1792]{1,0:T(8,128)(2,1)} %bitcast.14, bf16[224,1792]{1,0:T(8,128)(2,1)} %bitcast.10, bf16[224,512]{1,0:T(8,128)(2,1)} %bitcast.13, bf16[224,1792]{1,0:T(8,128)(2,1)} %bitcast.11, bf16[2432,1792]{1,0:T(8,128)(2,1)} %unembed.1, ...), custom_call_target="tpu_custom_call" | custom-call | tf_op jit(solution)/shard_map/pallas_call | solution.py:577
  229.9 1.3 slice_reduce_fusion.2
  231.2 0.7 slice_reduce_fusion.3
  231.9 0.7 reshape_squeeze.7
  232.6 1.6 copy.31
  (10 shorter events, 0.2 us)
